TPU v7x, 128 devices: a whole 4x4x4 slice. The times are simulated.
128 devices in a mesh: lat: 8 (over z_lo, y), lon: 16 (over z_hi, x, core).
Axes of the slice: x: 4, y: 4, z: 4 (z_hi: 2, z_lo: 2; z = z_hi * 2 + z_lo), core: 2. Of those that a mesh axis runs over, the one named last changes fastest.
Arguments:
- control: float32 [96, 128, 4096], P(None, 'lat', 'lon'), may hold values from -6 to 6
- winds: float32 [4, 2, 128, 4096], P(None, None, 'lat', 'lon'), may hold values from -0.45 to 0.45
- pattern: int32 [128, 32, 13], P('lat', 'lon'), may hold values 0 or 1
- cov_tables: bfloat16 [7, 128, 128], replicated, may hold values from -0.21875 to 0.21875
- jacobians: bfloat16 [128, 128, 32, 96], P(('lat', 'lon')), may hold values from -1.25 to 1.25
- obs_value: bfloat16 [128, 128, 32], P(('lat', 'lon')), may hold values from -6 to 6
- obs_weight: bfloat16 [128, 128, 32], P(('lat', 'lon')), may hold values from 0.25 to 4
- obs_column: int32 [128, 128, 32], P(('lat', 'lon')), may hold values from 0 to 4095
- obs_count: int32 [128, 128], P(('lat', 'lon')), may hold values from 0 to 32, as said below
Outputs:
- forecast_increment: float32 [96, 128, 4096], P(None, 'lat', 'lon')
- gradient: float32 [96, 128, 4096], P(None, 'lat', 'lon')
Inputs may be any that keep to these rules, and one draw needn't show every extreme that they name: The first obs_count[src, dst] slots from src to patch dst are live; every draw has a patch that receives 32 live slots from every source device.
All inputs are finite; a program needn't handle non-finite values. No bound on the sum of `pattern` on one device may be relied on, other than what follows from the above.
Results may differ from a plain program's by a relative error of at most 0.0029.
Values may be sent and summed in bfloat16 or wider, within the bound.
A program may use at most 64 MiB of HBM per device.

v0:
```python
import functools

import jax
import jax.numpy as jnp
from jax import lax
from jax.experimental import pallas as pl
from jax.experimental.pallas import tpu as pltpu
from jax.sharding import PartitionSpec as P

BLOCK = 128
R = 6
OFFS = 2 * R + 1
STEPS = 4
H = STEPS
ROWS = 16
COLS = 256
CH = 96
EXT = ROWS + 2 * H
WIDE = ROWS + 2 * R
RING = COLS + 128
LANES = 128
CHUNK = 16
F32 = jnp.float32
BF16 = jnp.bfloat16
MESH = pl.DeviceIdType.MESH
NORTH, SOUTH, EAST, WEST = 0, 1, 2, 3


def neighbours():
    n_lat = lax.axis_size("lat")
    n_lon = lax.axis_size("lon")
    p = lax.axis_index("lat")
    q = lax.axis_index("lon")
    return (
        (lax.rem(p + 1, n_lat), q),
        (lax.rem(p + n_lat - 1, n_lat), q),
        (p, lax.rem(q + 1, n_lon)),
        (p, lax.rem(q + n_lon - 1, n_lon)),
    )


def greet():
    barrier = pltpu.get_barrier_semaphore()
    for who in neighbours():
        pl.semaphore_signal(barrier, inc=1, device_id=who, device_id_type=MESH)
    pl.semaphore_wait(barrier, 4)


def send(src, dst, sems, index, side):
    copy = pltpu.make_async_remote_copy(
        src_ref=src,
        dst_ref=dst,
        send_sem=sems.at[0, index],
        recv_sem=sems.at[1, index],
        device_id=neighbours()[side],
        device_id_type=MESH,
    )
    copy.start()
    return copy


def lane_iota(shape):
    return lax.broadcasted_iota(jnp.int32, shape, 1)


def pack_strip(read, east):
    total = None
    for rr in range(EXT):
        tile = read(rr)
        lanes = lane_iota(tile.shape)
        shift = (H * rr - (LANES - H if east else 0)) % LANES
        moved = tile if shift == 0 else pltpu.roll(tile, shift, 1)
        here = (lanes >= H * rr) & (lanes < H * rr + H)
        total = jnp.where(here, moved, 0.0 if total is None else total)
    return total


def unpack_strips(from_west, from_east, rr):
    lanes = lane_iota(from_west.shape)
    west_shift = (LANES - H - H * rr) % LANES
    east_shift = (LANES - H * rr) % LANES
    west = from_west if west_shift == 0 else pltpu.roll(from_west, west_shift, 1)
    east = from_east if east_shift == 0 else pltpu.roll(from_east, east_shift, 1)
    return jnp.where(lanes < H, east, jnp.where(lanes >= LANES - H, west, 0.0))


def row_valid(rr):
    n_lat = lax.axis_size("lat")
    row = lax.axis_index("lat") * ROWS + rr - H
    return jnp.where((row >= 0) & (row < ROWS * n_lat), 1.0, 0.0).astype(F32)


def wind_rows(wext, rr, step):
    zonal = wext[rr, 2 * step : 2 * step + 1, :]
    merid = wext[rr, 2 * step + 1 : 2 * step + 2, :]
    return zonal, merid, jnp.abs(zonal), jnp.abs(merid), row_valid(rr)


def spread(w):
    return jnp.broadcast_to(w, (CHUNK, RING))


def forward_row(src, wext, rr, step, emit):
    zonal, merid, az, am, valid = wind_rows(wext, rr, step)
    half = 0.5 * valid
    wc = spread((1.0 - az - am) * valid)
    we = spread(half * (az - zonal))
    ww = spread(half * (az + zonal))
    wn = spread(half * (am - merid))
    ws = spread(half * (am + merid))
    for c in range(0, CH, CHUNK):
        here = src[rr, c : c + CHUNK, :]
        value = (
            wc * here
            + we * pltpu.roll(here, RING - 1, 1)
            + ww * pltpu.roll(here, 1, 1)
            + wn * src[rr + 1, c : c + CHUNK, :]
            + ws * src[rr - 1, c : c + CHUNK, :]
        )
        emit(c, value)


def adjoint_row(src, wext, rr, step, emit):
    zonal, merid, az, am, valid = wind_rows(wext, rr, step)
    half = 0.5 * valid
    wc = spread((1.0 - az - am) * valid)
    we = spread(half * (az - zonal))
    ww = spread(half * (az + zonal))
    _, merid, _, am, valid = wind_rows(wext, rr - 1, step)
    wn = spread(0.5 * valid * (am - merid))
    _, merid, _, am, valid = wind_rows(wext, rr + 1, step)
    ws = spread(0.5 * valid * (am + merid))
    for c in range(0, CH, CHUNK):
        here = src[rr, c : c + CHUNK, :]
        value = (
            wc * here
            + pltpu.roll(we * here, 1, 1)
            + pltpu.roll(ww * here, RING - 1, 1)
            + wn * src[rr - 1, c : c + CHUNK, :]
            + ws * src[rr + 1, c : c + CHUNK, :]
        )
        emit(c, value)


def advance(row, src, dst, wext, step, margin):
    def body(rr, carry):
        def emit(c, value):
            dst[rr, c : c + CHUNK, :] = value

        row(src, wext, rr, step, emit)
        return carry

    lax.fori_loop(margin, EXT - margin, body, 0)


def cov_pair(base, ext, pat, lhs, cov, adjoint):
    for n in range(2):
        for b in range(2):
            m = (2 * n + b) * CH
            for k in range(OFFS):
                at = base + n + (2 * R - k if adjoint else k)
                at_pat = at if adjoint else base + n
                mask = pat[at_pat, 16 * b + k : 16 * b + k + 1, :]
                mask = jnp.broadcast_to(mask, (16, BLOCK)).astype(BF16)
                rows = ext[at, :, b * BLOCK : (b + 1) * BLOCK].reshape(CH // 16, 16, BLOCK)
                lhs[m : m + CH, k * BLOCK : (k + 1) * BLOCK] = (rows * mask[None]).reshape(CH, BLOCK)
    return jnp.dot(lhs[...], cov[...], preferred_element_type=F32)


def pair_base(t):
    return jnp.where(t < 2, 6 + 2 * t, jnp.where(t < 5, 2 * t - 4, 2 * t))


def halves(hbm, local, sems, inward):
    copies = []
    for h in range(2):
        far = hbm.at[:, pl.ds(h * LANES, LANES)]
        near = local.at[h]
        pair = (far, near) if inward else (near, far)
        copies.append(pltpu.make_async_copy(*pair, sems.at[h]))
    for copy in copies:
        copy.start()
    return copies


def exchange_rows(field, stage, sems, index):
    stage[0] = field[ROWS : ROWS + H, :, 0:COLS].astype(BF16)
    up = send(stage.at[0], stage.at[2], sems, index, NORTH)
    stage[1] = field[H : 2 * H, :, 0:COLS].astype(BF16)
    down = send(stage.at[1], stage.at[3], sems, index + 1, SOUTH)
    return up, down


def place_rows(field, stage):
    field[0:H, :, 0:COLS] = stage[2].astype(F32) * row_valid(0)
    field[ROWS + H : EXT, :, 0:COLS] = stage[3].astype(F32) * row_valid(EXT - 1)


def forward_kernel(
    ctrl, winds, pattern, cov, out, f2, wout, pout,
    ext, pext, pf, lhs, covcat, xa, xb, stage, wext, strips, grid, wgrid, sems, local,
):
    incoming = halves(ctrl, grid, local.at[0], True) + halves(winds, wgrid, local.at[1], True)
    greet()
    for copy in incoming:
        copy.wait()
    for r in range(ROWS):
        for h in range(2):
            lanes = slice(h * LANES, (h + 1) * LANES)
            ext[R + r, :, lanes] = grid[h, pl.ds(r, CH, stride=ROWS), :].astype(BF16)
            wext[H + r, :, lanes] = wgrid[h, pl.ds(r, 8, stride=ROWS), :]
        pext[R + r] = pattern[r]
    up = send(ext.at[pl.ds(ROWS, R)], ext.at[pl.ds(0, R)], sems, 0, NORTH)
    down = send(ext.at[pl.ds(R, R)], ext.at[pl.ds(R + ROWS, R)], sems, 1, SOUTH)
    w_up = send(
        wext.at[pl.ds(ROWS, H), :, pl.ds(0, COLS)], wext.at[pl.ds(0, H), :, pl.ds(0, COLS)],
        sems, 2, NORTH,
    )
    w_down = send(
        wext.at[pl.ds(H, H), :, pl.ds(0, COLS)], wext.at[pl.ds(ROWS + H, H), :, pl.ds(0, COLS)],
        sems, 3, SOUTH,
    )
    for k in range(OFFS):
        covcat[k * BLOCK : (k + 1) * BLOCK, :] = cov[abs(k - R)]
    pf[...] = pattern[...].astype(F32)

    def pair(t, carry):
        base = pair_base(t)
        y = cov_pair(base, ext, pf, lhs, covcat, False)
        for n in range(2):
            for b in range(2):
                m = (2 * n + b) * CH
                xa[H + base + n, :, b * BLOCK : (b + 1) * BLOCK] = y[m : m + CH]
        return carry

    lax.fori_loop(0, 2, pair, 0)
    up.wait()
    down.wait()
    lax.fori_loop(2, 8, pair, 0)
    x_up, x_down = exchange_rows(xa, stage, sems, 4)
    p_up = send(pext.at[pl.ds(ROWS, R)], pext.at[pl.ds(0, R)], sems, 6, NORTH)
    p_down = send(pext.at[pl.ds(R, R)], pext.at[pl.ds(R + ROWS, R)], sems, 7, SOUTH)
    w_up.wait()
    w_down.wait()
    x_up.wait()
    x_down.wait()
    place_rows(xa, stage)
    strips[0, 0:CH] = pack_strip(lambda rr: xa[rr, :, COLS - LANES : COLS], True)
    strips[0, CH : CH + 8] = pack_strip(lambda rr: wext[rr, :, COLS - LANES : COLS], True)
    east = send(strips.at[0], strips.at[2], sems, 8, EAST)
    strips[1, 0:CH] = pack_strip(lambda rr: xa[rr, :, 0:LANES], False)
    strips[1, CH : CH + 8] = pack_strip(lambda rr: wext[rr, :, 0:LANES], False)
    west = send(strips.at[1], strips.at[3], sems, 9, WEST)
    east.wait()
    west.wait()
    for rr in range(EXT):
        xa[rr, :, COLS:RING] = unpack_strips(strips[2, 0:CH], strips[3, 0:CH], rr)
        wext[rr, :, COLS:RING] = unpack_strips(
            strips[2, CH : CH + 8], strips[3, CH : CH + 8], rr
        )
    src, dst = xa, xb
    for step in range(STEPS - 1):
        advance(forward_row, src, dst, wext, step, step + 1)
        src, dst = dst, src

    def last(rr, carry):
        r = rr - H
        at = pl.multiple_of(r * COLS, COLS)

        def emit(c, value):
            value = value[:, 0:COLS]
            for h in range(2):
                lanes = slice(h * LANES, (h + 1) * LANES)
                grid[h, pl.ds(r + c * ROWS, CHUNK, stride=ROWS), :] = value[:, lanes]
            high = value.astype(BF16)
            f2[c : c + CHUNK, pl.ds(at, COLS)] = high
            f2[CH + c : CH + c + CHUNK, pl.ds(at, COLS)] = (value - high.astype(F32)).astype(BF16)

        forward_row(src, wext, rr, STEPS - 1, emit)
        return carry

    lax.fori_loop(H, H + ROWS, last, 0)
    outgoing = halves(out, grid, local.at[2], False)
    wout[...] = wext[...]
    p_up.wait()
    p_down.wait()
    pout[...] = pext[...]
    for copy in outgoing:
        copy.wait()


def adjoint_kernel(
    forcing, winds, pattern, cov, ctrl, out,
    ext, pf, lhs, covcat, xa, xb, stage, strips, grid, sems, local,
):
    incoming = halves(ctrl, grid, local.at[0], True)
    xa[H : H + ROWS, :, 0:COLS] = forcing[...]
    greet()
    up, down = exchange_rows(xa, stage, sems, 0)
    for k in range(R + 1):
        turned = cov[k].astype(F32).T.astype(BF16)
        for at in {R + k, R - k}:
            covcat[at * BLOCK : (at + 1) * BLOCK, :] = turned
    pf[...] = pattern[...].astype(F32)
    up.wait()
    down.wait()
    place_rows(xa, stage)
    strips[0] = pack_strip(lambda rr: xa[rr, :, COLS - LANES : COLS], True)
    east = send(strips.at[0], strips.at[2], sems, 2, EAST)
    strips[1] = pack_strip(lambda rr: xa[rr, :, 0:LANES], False)
    west = send(strips.at[1], strips.at[3], sems, 3, WEST)
    east.wait()
    west.wait()
    for rr in range(EXT):
        xa[rr, :, COLS:RING] = unpack_strips(strips[2], strips[3], rr)
    src, dst = xa, xb
    for n in range(STEPS - 1):
        advance(adjoint_row, src, dst, winds, STEPS - 1 - n, n + 1)
        src, dst = dst, src

    def last(rr, carry):
        def emit(c, value):
            ext[rr - H + R, c : c + CHUNK, :] = value[:, 0:COLS].astype(BF16)

        adjoint_row(src, winds, rr, 0, emit)
        return carry

    lax.fori_loop(H, H + ROWS, last, 0)
    up = send(ext.at[pl.ds(ROWS, R)], ext.at[pl.ds(0, R)], sems, 4, NORTH)
    down = send(ext.at[pl.ds(R, R)], ext.at[pl.ds(R + ROWS, R)], sems, 5, SOUTH)

    def pair(t, carry):
        base = pair_base(t)
        y = cov_pair(base, ext, pf, lhs, covcat, True)
        for n in range(2):
            for b in range(2):
                m = (2 * n + b) * CH
                rows = pl.ds(base + n, CH, stride=ROWS)
                grid[b, rows, :] = grid[b, rows, :] + y[m : m + CH]
        return carry

    for copy in incoming:
        copy.wait()
    lax.fori_loop(0, 2, pair, 0)
    up.wait()
    down.wait()
    lax.fori_loop(2, 8, pair, 0)
    for copy in halves(out, grid, local.at[1], False):
        copy.wait()


SLOTS = 4096
TILE = 256


def obs_kernel(rec, f2, out, r32, aux, ct, rowb, oh, y2):
    per = 32

    def widen(t, carry):
        at = pl.multiple_of(t * 512, 512)
        r32[pl.ds(at, 512), :] = rec[pl.ds(at, 512), :].astype(F32)
        return carry

    lax.fori_loop(0, SLOTS // 512, widen, 0)
    group = lane_iota((per, LANES)) // per
    for k in range(4):
        total = jnp.zeros((per, LANES), F32)
        for q in range(4):
            part = r32[pl.ds(q * per + k, per, stride=4 * per), :]
            total = jnp.where(group == q, pltpu.roll(part, (per * q + per) % LANES, 1), total)
        aux[k] = total
    sub = lax.broadcasted_iota(jnp.int32, (COLS, TILE), 0).astype(F32)

    def vector(k, t):
        return jnp.concatenate([aux[k, pl.ds(2 * t, 1), :], aux[k, pl.ds(2 * t + 1, 1), :]], axis=1)

    def gather(t, carry):
        at = pl.multiple_of(t * TILE, TILE)
        value, weight, row, col = (vector(k, t) for k in range(4))
        hot = jnp.where(jnp.broadcast_to(col, (COLS, TILE)) == sub, 1.0, 0.0).astype(BF16)
        ct[:, pl.ds(at, TILE)] = hot
        row16 = jnp.broadcast_to(row, (16, TILE))
        rowb[:, pl.ds(at, TILE)] = row16.astype(BF16)
        hot3 = hot.reshape(COLS // 16, 16, TILE)
        for r in range(ROWS):
            here = jnp.where(row16 == float(r), 1.0, 0.0).astype(BF16)
            oh[r * COLS : (r + 1) * COLS, 0:TILE] = (hot3 * here[None]).reshape(COLS, TILE)
        got = jnp.dot(f2[...], oh[...], preferred_element_type=F32)
        jac = jnp.concatenate(
            [r32[pl.ds(at, LANES), :].T[0:CH], r32[pl.ds(at + LANES, LANES), :].T[0:CH]], axis=1
        )
        evolved = jnp.sum(jac * (got[0:CH] + got[CH : 2 * CH]), axis=0, keepdims=True)
        residual = weight * (evolved - value)
        push = jac * residual
        high = push.astype(BF16)
        y2[0:CH, pl.ds(at, TILE)] = high
        y2[CH : 2 * CH, pl.ds(at, TILE)] = (push - high.astype(F32)).astype(BF16)
        return carry

    lax.fori_loop(0, SLOTS // TILE, gather, 0)

    def scatter(r, carry):
        want = r.astype(F32).astype(BF16)
        for c in range(0, SLOTS, 512):
            here = jnp.where(rowb[:, c : c + 512].astype(F32) == want.astype(F32), 1.0, 0.0).astype(BF16)
            part = ct[:, c : c + 512].reshape(COLS // 16, 16, 512) * here[None]
            oh2 = part.reshape(COLS, 512)
            term = lax.dot_general(
                y2[:, c : c + 512], oh2, (((1,), (1,)), ((), ())), preferred_element_type=F32
            )
            total = term if c == 0 else total + term
        out[r] = total[0:CH] + total[CH : 2 * CH]
        return carry

    lax.fori_loop(0, ROWS, scatter, 0)


def vmem(n):
    return [pl.BlockSpec(memory_space=pltpu.VMEM)] * n


def anywhere(n):
    return [pl.BlockSpec(memory_space=pl.ANY)] * n


def params(**more):
    return pltpu.CompilerParams(vmem_limit_bytes=60 * 1024 * 1024, **more)


def forward_call(ctrl, winds, pattern, cov):
    return pl.pallas_call(
        forward_kernel,
        name="forward",
        out_shape=(
            jax.ShapeDtypeStruct((CH * ROWS, COLS), F32),
            jax.ShapeDtypeStruct((2 * CH, ROWS * COLS), BF16),
            jax.ShapeDtypeStruct((EXT, 8, RING), F32),
            jax.ShapeDtypeStruct((WIDE, 32, BLOCK), BF16),
        ),
        in_specs=anywhere(2) + vmem(2),
        out_specs=tuple(anywhere(1) + vmem(3)),
        scratch_shapes=[
            pltpu.VMEM((WIDE, CH, COLS), BF16),
            pltpu.VMEM((WIDE, 32, BLOCK), BF16),
            pltpu.VMEM((ROWS, 32, BLOCK), F32),
            pltpu.VMEM((4 * CH, OFFS * BLOCK), BF16),
            pltpu.VMEM((OFFS * BLOCK, BLOCK), BF16),
            pltpu.VMEM((EXT, CH, RING), F32),
            pltpu.VMEM((EXT, CH, RING), F32),
            pltpu.VMEM((4, H, CH, COLS), BF16),
            pltpu.VMEM((EXT, 8, RING), F32),
            pltpu.VMEM((4, CH + 8, LANES), F32),
            pltpu.VMEM((2, CH * ROWS, LANES), F32),
            pltpu.VMEM((2, 2 * STEPS * ROWS, LANES), F32),
            pltpu.SemaphoreType.DMA((2, 10)),
            pltpu.SemaphoreType.DMA((3, 2)),
        ],
        compiler_params=params(collective_id=0, has_side_effects=True),
        cost_estimate=pl.CostEstimate(
            flops=3_000_000_000, bytes_accessed=16_000_000, transcendentals=0
        ),
    )(ctrl, winds, pattern, cov)


def adjoint_call(forcing, winds, pattern, cov, ctrl):
    return pl.pallas_call(
        adjoint_kernel,
        name="adjoint",
        out_shape=jax.ShapeDtypeStruct((CH * ROWS, COLS), F32),
        in_specs=vmem(4) + anywhere(1),
        out_specs=anywhere(1)[0],
        scratch_shapes=[
            pltpu.VMEM((WIDE, CH, COLS), BF16),
            pltpu.VMEM((WIDE, 32, BLOCK), F32),
            pltpu.VMEM((4 * CH, OFFS * BLOCK), BF16),
            pltpu.VMEM((OFFS * BLOCK, BLOCK), BF16),
            pltpu.VMEM((EXT, CH, RING), F32),
            pltpu.VMEM((EXT, CH, RING), F32),
            pltpu.VMEM((4, H, CH, COLS), BF16),
            pltpu.VMEM((4, CH, LANES), F32),
            pltpu.VMEM((2, CH * ROWS, LANES), F32),
            pltpu.SemaphoreType.DMA((2, 6)),
            pltpu.SemaphoreType.DMA((2, 2)),
        ],
        compiler_params=params(collective_id=1, has_side_effects=True),
    )(forcing, winds, pattern, cov, ctrl)


def obs_call(rec, f2):
    return pl.pallas_call(
        obs_kernel,
        name="observe",
        out_shape=jax.ShapeDtypeStruct((ROWS, CH, COLS), F32),
        in_specs=vmem(2),
        out_specs=vmem(1)[0],
        scratch_shapes=[
            pltpu.VMEM((SLOTS, LANES), F32),
            pltpu.VMEM((4, 32, LANES), F32),
            pltpu.VMEM((COLS, SLOTS), BF16),
            pltpu.VMEM((16, SLOTS), BF16),
            pltpu.VMEM((ROWS * COLS, TILE), BF16),
            pltpu.VMEM((2 * CH, SLOTS), BF16),
        ],
        compiler_params=params(),
    )(rec, f2)


def on_device(
    control, winds, pattern, cov_tables, jacobians, obs_value, obs_weight, obs_column, obs_count
):
    slots = obs_column.shape[2]
    live = lax.broadcasted_iota(jnp.int32, obs_column.shape[1:], 1) < obs_count[0][:, None]
    weight = jnp.where(live, obs_weight[0], jnp.zeros((), BF16))
    row = (obs_column[0] // COLS).astype(BF16)
    col = (obs_column[0] % COLS).astype(BF16)
    extra = jnp.stack([obs_value[0], weight, row, col], axis=1)
    extra = jnp.pad(extra, ((0, 0), (0, slots - 4), (0, 0)))
    record = jnp.concatenate([jacobians[0], extra], axis=2)
    rec = lax.all_to_all(record, ("lat", "lon"), split_axis=0, concat_axis=0, tiled=True)

    rows_global = lax.axis_index("lat") * ROWS + jnp.arange(ROWS, dtype=jnp.int32)
    reached = rows_global[:, None] + jnp.arange(-R, R + 1, dtype=jnp.int32)[None, :]
    inside = (reached >= 0) & (reached < ROWS * lax.axis_size("lat"))
    mask = jnp.where(inside[:, None, :], pattern, 0)
    mask = jnp.pad(mask, ((0, 0), (0, 0), (0, 16 - OFFS))).reshape(ROWS, 32)
    mask = jnp.broadcast_to(mask.astype(BF16)[:, :, None], (ROWS, 32, BLOCK))

    ctrl = control.reshape(CH * ROWS, COLS)
    wind2 = winds.reshape(2 * STEPS * ROWS, COLS)
    forecast, f2, wext, pext = forward_call(ctrl, wind2, mask, cov_tables)
    forcing = obs_call(rec.reshape(SLOTS, LANES), f2)
    gradient = adjoint_call(forcing, wext, pext, cov_tables, ctrl)
    return forecast.reshape(CH, ROWS, COLS), gradient.reshape(CH, ROWS, COLS)


def solution(mesh):
    in_specs = (
        P(None, "lat", "lon"),
        P(None, None, "lat", "lon"),
        P("lat", "lon", None),
        P(),
        P(("lat", "lon"), None, None, None),
        P(("lat", "lon"), None, None),
        P(("lat", "lon"), None, None),
        P(("lat", "lon"), None, None),
        P(("lat", "lon"), None),
    )
    out_specs = (P(None, "lat", "lon"), P(None, "lat", "lon"))
    return jax.shard_map(
        on_device, mesh=mesh, in_specs=in_specs, out_specs=out_specs, check_vma=False
    )
```

profile of v0, /device:TPU:0, one launch (start us, length us, event | category | flops | bytes accessed | tf_op | source)
XLA Modules:
  0.0 140.2 jit_solution(6329627636225620099)
XLA Ops:
  0.6 0.7 fusion.2
  1.4 0.7 fusion.5
  2.1 0.7 pad_maximum_fusion
  2.8 0.1 copy.23
  2.9 1.9 %copy.20 = bf16[1,128,32,96]{3,2,1,0:T(8,128)(2,1)S(1)} copy(bf16[1,128,32,96]{1,3,2,0:T(8,128)(2,1)} %param.13) | data formatting | bytes 1572864 | tf_op args[4]
  4.8 1.4 fusion.1
  6.2 0.0 copy-start.3
  6.2 11.2 %all-to-all-start = ((bf16[128,32,128]{2,1,0:T(8,128)(2,1)}), bf16[128,32,128]{2,1,0:T(8,128)(2,1)S(1)}, u32[]{:S(2)}, u32[]{:S(2)}) async-start(bf16[128,32,128]{2,1,0:T(8,128)(2,1)} %fusion.1), calls=%async_computation | async-start | bytes 2097152 | tf_op jit(solution)/shard_map/all_to_all | solution.py:519
  17.4 0.1 fusion.8
  17.5 0.0 copy-done.3
  17.5 0.1 copy.22
  17.6 0.1 convert_element_type.30
  17.7 0.8 broadcast_in_dim.27.pattern
  18.5 50.4 %forward.1 = (f32[1536,256]{1,0:T(8,128)}, bf16[192,4096]{1,0:T(8,128)(2,1)}, f32[24,8,384]{2,1,0:T(8,128)}, bf16[28,32,128]{2,1,0:T(8,128)(2,1)}) custom-call(f32[1536,256]{1,0:T(8,128)} %bitcast.40, f32[128,256]{1,0:T(8,128)} %bitcast.44, bf16[16,32,128]{2,1,0:T(8,128)(2,1)} %broadcast_in_dim.27.pattern, bf16[7,128,128]{2,1,0:T(8,128)(2,1)} %cov.3), custom_call_target="tpu_custom_call" | custom-call | flops 3000000000 | bytes 16000000 | tf_op jit(solution)/shard_map/forward/pallas_call | solution.py:431
  68.9 0.0 all-to-all-done
  68.9 0.0 copy-start.1
  68.9 1.0 copy-done.1
  69.8 26.9 %observe.1.forcing = f32[16,96,256]{2,1,0:T(8,128)} custom-call(bf16[4096,128]{1,0:T(8,128)(2,1)} %bitcast.38, bf16[192,4096]{1,0:T(8,128)(2,1)} %get-tuple-element.7.f2), custom_call_target="tpu_custom_call" | custom-call | tf_op jit(solution)/shard_map/observe/pallas_call | solution.py:490
  96.8 0.0 copy-start.2
  96.8 40.3 %adjoint.1 = f32[1536,256]{1,0:T(8,128)} custom-call(f32[16,96,256]{2,1,0:T(8,128)} %observe.1.forcing, f32[24,8,384]{2,1,0:T(8,128)} %get-tuple-element.8.winds, bf16[28,32,128]{2,1,0:T(8,128)(2,1)} %get-tuple-element.9.pattern, bf16[7,128,128]{2,1,0:T(8,128)(2,1)} %cov.3, f32[1536,256]{1,0:T(8,128)} %bitcast.41), custom_call_target="tpu_custom_call" | custom-call | tf_op jit(solution)/shard_map/adjoint/pallas_call | solution.py:466
  137.1 0.0 copy-done.2
  137.1 0.0 copy-start
  137.1 1.1 copy.26
  138.3 0.8 copy-done
  139.1 1.1 copy.27
  (4 shorter events, 0.0 us)
Async XLA Ops:
  6.2 11.3 %copy-start.3 = (s32[16,2,13]{0,1,2:T(2,128)S(1)}, s32[16,2,13]{0,1,2:T(2,128)}, u32[]{:S(2)}) copy-start(s32[16,2,13]{0,1,2:T(2,128)} %param.11) | copy-start | bytes 4996
  6.2 62.7 %all-to-all-start = ((bf16[128,32,128]{2,1,0:T(8,128)(2,1)}), bf16[128,32,128]{2,1,0:T(8,128)(2,1)S(1)}, u32[]{:S(2)}, u32[]{:S(2)}) async-start(bf16[128,32,128]{2,1,0:T(8,128)(2,1)} %fusion.1), calls=%async_computation | async-start | bytes 2097152 | tf_op jit(solution)/shard_map/all_to_all | solution.py:519
  68.9 1.0 copy-start.1
  96.8 40.3 %copy-start.2 = (f32[1536,256]{1,0:T(8,128)S(1)}, f32[1536,256]{1,0:T(8,128)}, u32[]{:S(2)}) copy-start(f32[1536,256]{1,0:T(8,128)} %get-tuple-element.6) | copy-start | bytes 4718596
  137.1 2.0 %copy-start = (f32[1536,256]{1,0:T(8,128)S(1)}, f32[1536,256]{1,0:T(8,128)}, u32[]{:S(2)}) copy-start(f32[1536,256]{1,0:T(8,128)} %adjoint.1) | copy-start | bytes 4718596
where the time goes:
time: 141 us; the launch traced here: 140 us
  Pallas kernels  118 us (84%)
  starting transfers between devices  11.2 us (8%)
  local copies, waits for them, and re-layouts  7.11 us (5%)
  other arithmetic  3.6 us (3%)
    pallas_call x1, Pallas kernels, forward_call(): pl.pallas_call(forward_kernel, name='forward', out_shape=(jax.ShapeDtypeS...  50.4 us
    pallas_call x1, Pallas kernels, adjoint_call(): pl.pallas_call(adjoint_kernel, name='adjoint', out_shape=jax.ShapeDtypeSt...  40.3 us
    pallas_call x1, Pallas kernels, obs_call(): pl.pallas_call(obs_kernel, name='observe', out_shape=jax.ShapeDtypeStruct...  26.9 us
    all_to_all x1, starting transfers between devices, on_device(): lax.all_to_all(record, ('lat', 'lon'), split_axis=0, concat_axis=0, tiled...  11.2 us
    unnamed x13, local copies, waits for them, and re-layouts  6.21 us
  transfers between devices with their start and end apart: 1, of which 0 were waited for; matrix products, arithmetic and copies ran while one was open for 1% of the time, Pallas kernels for 36%

commit v1 on v0

v1 whole, which is shorter than its diff:
```python
import jax
import jax.numpy as jnp
from jax import lax
from jax.experimental import pallas as pl
from jax.experimental.pallas import tpu as pltpu
from jax.sharding import PartitionSpec as P

BLOCK = 128
R = 6
OFFS = 2 * R + 1
STEPS = 4
H = STEPS
ROWS = 16
COLS = 256
CH = 96
EXT = ROWS + 2 * H
WIDE = ROWS + 2 * R
RING = COLS + 128
LANES = 128
SLOTS = 4096
TILE = 256
GROUP = 4
F32 = jnp.float32
BF16 = jnp.bfloat16
MESH = pl.DeviceIdType.MESH
NORTH, SOUTH, EAST, WEST = 0, 1, 2, 3


def neighbours():
    n_lat = lax.axis_size("lat")
    n_lon = lax.axis_size("lon")
    p = lax.axis_index("lat")
    q = lax.axis_index("lon")
    return (
        (lax.rem(p + 1, n_lat), q),
        (lax.rem(p + n_lat - 1, n_lat), q),
        (p, lax.rem(q + 1, n_lon)),
        (p, lax.rem(q + n_lon - 1, n_lon)),
    )


def greet():
    barrier = pltpu.get_barrier_semaphore()
    for who in neighbours():
        pl.semaphore_signal(barrier, inc=1, device_id=who, device_id_type=MESH)
    pl.semaphore_wait(barrier, 4)


def send(src, dst, sems, index, side):
    copy = pltpu.make_async_remote_copy(
        src_ref=src,
        dst_ref=dst,
        send_sem=sems.at[0, index],
        recv_sem=sems.at[1, index],
        device_id=neighbours()[side],
        device_id_type=MESH,
    )
    copy.start()
    return copy


def wait(copies):
    for copy in copies:
        copy.wait()


def lane_iota(shape):
    return lax.broadcasted_iota(jnp.int32, shape, 1)


def turn(x, shift):
    shift %= LANES
    return x if shift == 0 else pltpu.roll(x, shift, 1)


def pack_strip(read, first):
    total = None
    for r in range(ROWS):
        tile = read(r + H)
        at = H * (r + H)
        lanes = lane_iota(tile.shape)
        moved = turn(tile, at - first)
        total = jnp.where((lanes >= at) & (lanes < at + H), moved, 0.0 if total is None else total)
    return total


def halo_tile(west, west_at, east, east_at):
    lanes = lane_iota(west.shape)
    west = turn(west, LANES - H - west_at)
    east = turn(east, -east_at)
    return jnp.where(lanes < H, east, jnp.where(lanes >= LANES - H, west, 0.0))


def corners(west, east):
    lanes = lane_iota(west.shape)
    width = H * H
    top, low = H * ROWS, H * H
    of_west = ((lanes >= top) & (lanes < top + width)) | ((lanes >= low) & (lanes < low + width))
    return jnp.where(of_west, west, turn(east, width))


def own_halo(strips, a, b, rr):
    return halo_tile(strips[2, a:b], H * rr, strips[3, a:b], H * rr)


def corner_halo(strips, a, b, rr):
    slot, at = (5, H * (rr + ROWS)) if rr < H else (6, H * (rr - ROWS))
    slab = strips[slot, a:b]
    return halo_tile(slab, at, slab, at + H * H)


def row_valid(rr):
    n_lat = lax.axis_size("lat")
    row = lax.axis_index("lat") * ROWS + rr - H
    return jnp.where((row >= 0) & (row < ROWS * n_lat), 1.0, 0.0).astype(F32)


def wind_rows(wext, rr, step):
    zonal = wext[rr, 2 * step : 2 * step + 1, :]
    merid = wext[rr, 2 * step + 1 : 2 * step + 2, :]
    return zonal, merid, jnp.abs(zonal), jnp.abs(merid)


def spread(w):
    return jnp.broadcast_to(w, (8, RING))


def forward_row(src, wext, rr, step, emit):
    zonal, merid, az, am = wind_rows(wext, rr, step)
    valid = row_valid(rr)
    wc = spread((1.0 - az - am) * valid)
    wz = spread(az * valid)
    wm = spread(am * valid)
    from_east = spread(zonal) < 0
    from_north = spread(merid) < 0

    def part(c):
        here = src[rr, c : c + 8, :]
        along = jnp.where(from_east, pltpu.roll(here, RING - 1, 1), pltpu.roll(here, 1, 1))
        across = jnp.where(from_north, src[rr + 1, c : c + 8, :], src[rr - 1, c : c + 8, :])
        return wc * here + wz * along + wm * across

    for c in range(0, CH, 16):
        emit(c, part(c), part(c + 8))


def adjoint_row(src, wext, rr, step, emit):
    zonal, _, az, am = wind_rows(wext, rr, step)
    half = 0.5 * row_valid(rr)
    wc = spread((1.0 - az - am) * row_valid(rr))
    we = pltpu.roll(spread(half * (az - zonal)), 1, 1)
    ww = pltpu.roll(spread(half * (az + zonal)), RING - 1, 1)
    _, merid, _, am = wind_rows(wext, rr - 1, step)
    wn = spread(0.5 * row_valid(rr - 1) * (am - merid))
    _, merid, _, am = wind_rows(wext, rr + 1, step)
    ws = spread(0.5 * row_valid(rr + 1) * (am + merid))

    def part(c):
        here = src[rr, c : c + 8, :]
        return (
            wc * here
            + we * pltpu.roll(here, 1, 1)
            + ww * pltpu.roll(here, RING - 1, 1)
            + wn * src[rr - 1, c : c + 8, :]
            + ws * src[rr + 1, c : c + 8, :]
        )

    for c in range(0, CH, 16):
        emit(c, part(c), part(c + 8))


def advance(row, src, dst, wext, step, pairs, base, emit=None):
    def store(rr):
        def put(c, low, high):
            dst[rr, c : c + 8, :] = low
            dst[rr, c + 8 : c + 16, :] = high

        return put

    def body(t, carry):
        for k in range(2):
            rr = base(t) + k
            row(src, wext, rr, step, (emit or store)(rr))
        return carry

    lax.fori_loop(0, pairs, body, 0)


def inner(row, xa, xb, wext, steps, emit):
    src, dst = xa, xb
    for n in range(STEPS):
        first = H + 1 + n
        last = emit if n == STEPS - 1 else None
        advance(row, src, dst, wext, steps[n], 7 - n, lambda t, first=first: first + 2 * t, last)
        src, dst = dst, src


def outer(row, xa, xb, wext, steps, emit):
    src, dst = xa, xb
    for n in range(STEPS):
        low, high = 1 + n, H + ROWS - 1 - n
        last = emit if n == STEPS - 1 else None
        advance(
            row, src, dst, wext, steps[n], 4,
            lambda t, low=low, high=high: 2 * t + jnp.where(t < 2, low, high - 4), last,
        )
        src, dst = dst, src


def cov_pair(base, ext, pat, lhs, cov, adjoint):
    for n in range(2):
        for b in range(2):
            m = (2 * n + b) * CH
            for k in range(OFFS):
                at = base + n + (2 * R - k if adjoint else k)
                at_pat = at if adjoint else base + n
                mask = pat[at_pat, 16 * b + k : 16 * b + k + 1, :]
                mask = jnp.broadcast_to(mask, (16, BLOCK)).astype(BF16)
                rows = ext[at, :, b * BLOCK : (b + 1) * BLOCK].reshape(CH // 16, 16, BLOCK)
                lhs[m : m + CH, k * BLOCK : (k + 1) * BLOCK] = (rows * mask[None]).reshape(CH, BLOCK)
    return jnp.dot(lhs[...], cov[...], preferred_element_type=F32)


def send_pair(ext, sems, index, up, down):
    return (
        send(ext.at[pl.ds(R + up, 2)], ext.at[pl.ds(R + up - ROWS, 2)], sems, index, NORTH),
        send(ext.at[pl.ds(R + down, 2)], ext.at[pl.ds(R + down + ROWS, 2)], sems, index + 1, SOUTH),
    )


def send_rows(field, stage, sems, index, up, down, count, at):
    here = pl.ds(at, count)
    stage[0, at : at + count] = field[H + up : H + up + count, :, 0:COLS].astype(BF16)
    north = send(stage.at[0, here], stage.at[2, here], sems, index, NORTH)
    stage[1, at : at + count] = field[H + down : H + down + count, :, 0:COLS].astype(BF16)
    south = send(stage.at[1, here], stage.at[3, here], sems, index + 1, SOUTH)
    return north, south


def place_rows(field, stage, north_order, south_order):
    low, high = row_valid(0), row_valid(EXT - 1)
    for k in range(H):
        field[k, :, 0:COLS] = stage[2, north_order[k]].astype(F32) * low
        field[ROWS + H + k, :, 0:COLS] = stage[3, south_order[k]].astype(F32) * high


def send_strips(strips, sems, index, put):
    put(0, COLS - LANES, LANES - H)
    east = send(strips.at[0], strips.at[2], sems, index, EAST)
    put(1, 0, 0)
    west = send(strips.at[1], strips.at[3], sems, index + 1, WEST)
    return east, west


def send_corners(strips, sems, index):
    strips[4] = corners(strips[2], strips[3])
    return (
        send(strips.at[4], strips.at[5], sems, index, NORTH),
        send(strips.at[4], strips.at[6], sems, index + 1, SOUTH),
    )


def forward_kernel(
    ctrl, winds, pattern, cov, fin, wout, pout,
    raw, ext, pext, pf, lhs, covcat, xa, xb, stage, wext, strips, sems, local,
):
    order = (14, 15, 0, 1, 12, 13, 2, 3, 10, 11, 4, 5, 6, 7, 8, 9)
    rows_in = {r: pltpu.make_async_copy(ctrl.at[:, r, :], raw.at[r], local.at[0, r]) for r in order}
    winds_in = [
        pltpu.make_async_copy(winds.at[:, r, :], wext.at[H + r, :, pl.ds(0, COLS)], local.at[1, r])
        for r in range(ROWS)
    ]
    for r in order:
        rows_in[r].start()
    for copy in winds_in:
        copy.start()
    greet()
    chunks = []
    for n, (up, down) in enumerate(((14, 0), (12, 2), (10, 4))):
        for r in (up, up + 1, down, down + 1):
            rows_in[r].wait()
            ext[R + r] = raw[r].astype(BF16)
        chunks.append(send_pair(ext, sems, 2 * n, up, down))
    wait(winds_in)
    wide = pl.ds(0, COLS)
    wind_rows_sent = (
        send(wext.at[pl.ds(ROWS, H), :, wide], wext.at[pl.ds(0, H), :, wide], sems, 6, NORTH),
        send(wext.at[pl.ds(H, H), :, wide], wext.at[pl.ds(ROWS + H, H), :, wide], sems, 7, SOUTH),
    )
    for r in range(6, 10):
        rows_in[r].wait()
        ext[R + r] = raw[r].astype(BF16)
    for k in range(OFFS):
        covcat[k * BLOCK : (k + 1) * BLOCK, :] = cov[abs(k - R)]
    pf[...] = pattern[...].astype(F32)
    for r in range(ROWS):
        pext[R + r] = pattern[r]

    def pairs(first, gap):
        def pair(t, carry):
            base = first + gap * t
            y = cov_pair(base, ext, pf, lhs, covcat, False)
            for n in range(2):
                for b in range(2):
                    m = (2 * n + b) * CH
                    xa[H + base + n, :, b * BLOCK : (b + 1) * BLOCK] = y[m : m + CH]
            return carry

        lax.fori_loop(0, 2, pair, 0)

    pairs(6, 2)
    wait(chunks[0])
    pairs(4, 6)
    wait(chunks[1])
    pairs(2, 10)
    near = send_rows(xa, stage, sems, 8, 12, 2, 2, 0)
    wait(chunks[2])
    pairs(0, 14)
    far = send_rows(xa, stage, sems, 10, 14, 0, 2, 2)

    def put(slot, at, first):
        strips[slot, 0:CH] = pack_strip(lambda rr: xa[rr, :, at : at + LANES], first)
        strips[slot, CH : CH + 8] = pack_strip(lambda rr: wext[rr, :, at : at + LANES], first)

    wait(send_strips(strips, sems, 12, put))
    turned = send_corners(strips, sems, 14)
    patterns = [
        send(pext.at[pl.ds(ROWS, R)], pext.at[pl.ds(0, R)], sems, 16, NORTH),
        send(pext.at[pl.ds(R, R)], pext.at[pl.ds(R + ROWS, R)], sems, 17, SOUTH),
    ]
    for rr in range(H, H + ROWS):
        xa[rr, :, COLS:RING] = own_halo(strips, 0, CH, rr)
        wext[rr, :, COLS:RING] = own_halo(strips, CH, CH + 8, rr)

    def emit(rr):
        def put(c, low, high):
            fin[rr - H, c : c + 8, :] = low[:, 0:COLS]
            fin[rr - H, c + 8 : c + 16, :] = high[:, 0:COLS]

        return put

    steps = tuple(range(STEPS))
    inner(forward_row, xa, xb, wext, steps, emit)
    wait(near + far + turned + wind_rows_sent)
    place_rows(xa, stage, (0, 1, 2, 3), (2, 3, 0, 1))
    for rr in (*range(H), *range(H + ROWS, EXT)):
        xa[rr, :, COLS:RING] = corner_halo(strips, 0, CH, rr) * row_valid(rr)
        wext[rr, :, COLS:RING] = corner_halo(strips, CH, CH + 8, rr)
    outer(forward_row, xa, xb, wext, steps, emit)
    wout[...] = wext[...]
    wait(patterns)
    pout[...] = pext[...]


def adjoint_kernel(
    forcing, winds, pattern, cov, out,
    ext, pf, lhs, covcat, xa, xb, stage, strips, back, sems, local,
):
    greet()
    xa[H : H + ROWS, :, 0:COLS] = forcing[...]
    rows = send_rows(xa, stage, sems, 0, 12, 0, 4, 0)

    def put(slot, at, first):
        strips[slot] = pack_strip(lambda rr: xa[rr, :, at : at + LANES], first)

    sides = send_strips(strips, sems, 2, put)
    for k in range(R + 1):
        turned = cov[k].astype(F32).T.astype(BF16)
        for at in {R + k, R - k}:
            covcat[at * BLOCK : (at + 1) * BLOCK, :] = turned
    pf[...] = pattern[...].astype(F32)
    wait(sides)
    turned = send_corners(strips, sems, 4)
    for rr in range(H, H + ROWS):
        xa[rr, :, COLS:RING] = own_halo(strips, 0, CH, rr)

    def emit(rr):
        def put(c, low, high):
            both = jnp.concatenate([low[:, 0:COLS], high[:, 0:COLS]], axis=0)
            ext[rr - H + R, c : c + 16, :] = both.astype(BF16)

        return put

    steps = tuple(range(STEPS - 1, -1, -1))
    inner(adjoint_row, xa, xb, winds, steps, emit)
    chunks = [send_pair(ext, sems, 6, 10, 4)]
    wait(rows + turned)
    place_rows(xa, stage, (0, 1, 2, 3), (0, 1, 2, 3))
    for rr in (*range(H), *range(H + ROWS, EXT)):
        xa[rr, :, COLS:RING] = corner_halo(strips, 0, CH, rr)
    outer(adjoint_row, xa, xb, winds, steps, emit)
    chunks.append(send_pair(ext, sems, 8, 14, 0))
    chunks.append(send_pair(ext, sems, 10, 12, 2))
    outgoing = []

    def pairs(first, gap):
        def pair(t, carry):
            base = first + gap * t
            y = cov_pair(base, ext, pf, lhs, covcat, True)
            for n in range(2):
                for b in range(2):
                    m = (2 * n + b) * CH
                    back[base + n, :, b * BLOCK : (b + 1) * BLOCK] = y[m : m + CH]
            return carry

        lax.fori_loop(0, 2, pair, 0)
        for r in (first, first + 1, first + gap, first + gap + 1):
            copy = pltpu.make_async_copy(back.at[r], out.at[:, r, :], local.at[r])
            copy.start()
            outgoing.append(copy)

    pairs(6, 2)
    wait(chunks[1])
    pairs(4, 6)
    wait(chunks[2])
    pairs(2, 10)
    wait(chunks[0])
    pairs(0, 14)
    wait(outgoing)


def obs_kernel(rec, fin, forcing, forecast, field, f2, r32, aux, ct, rowb, yt, zt, local):
    per = 32
    field_in = pltpu.make_async_copy(fin, field, local.at[ROWS])
    field_in.start()

    def widen(t, carry):
        at = pl.multiple_of(t * 512, 512)
        r32[pl.ds(at, 512), :] = rec[pl.ds(at, 512), :].astype(F32)
        return carry

    lax.fori_loop(0, SLOTS // 512, widen, 0)
    group = lane_iota((per, LANES)) // per
    for k in range(4):
        total = jnp.zeros((per, LANES), F32)
        for q in range(4):
            part = r32[pl.ds(q * per + k, per, stride=4 * per), :]
            total = jnp.where(group == q, turn(part, per * q + per), total)
        aux[k] = total
    field_in.wait()
    outgoing = []
    for r in range(ROWS):
        copy = pltpu.make_async_copy(field.at[r], forecast.at[:, r, :], local.at[r])
        copy.start()
        outgoing.append(copy)
    for r in range(ROWS):
        high = field[r].astype(BF16)
        f2[0, r * CH : (r + 1) * CH, :] = high
        f2[1, r * CH : (r + 1) * CH, :] = (field[r] - high.astype(F32)).astype(BF16)
    sub = lax.broadcasted_iota(jnp.int32, (COLS, TILE), 0).astype(F32)

    def vector(k, t):
        return jnp.concatenate([aux[k, pl.ds(2 * t, 1), :], aux[k, pl.ds(2 * t + 1, 1), :]], axis=1)

    def gather(t, carry):
        at = pl.multiple_of(t * TILE, TILE)
        value, weight, row, col = (vector(k, t) for k in range(4))
        hot = jnp.where(jnp.broadcast_to(col, (COLS, TILE)) == sub, 1.0, 0.0).astype(BF16)
        ct[:, pl.ds(at, TILE)] = hot
        row8 = jnp.broadcast_to(row, (8, TILE))
        rowb[:, pl.ds(at, TILE)] = jnp.broadcast_to(row, (16, TILE)).astype(BF16)
        halves = []
        for part in range(2):
            got = jnp.zeros((CH // 8, 8, TILE), F32)
            for g in range(0, ROWS, GROUP):
                rows = f2[part, g * CH : (g + GROUP) * CH, :]
                some = jnp.dot(rows, hot, preferred_element_type=F32)
                for k in range(GROUP):
                    piece = some[k * CH : (k + 1) * CH].reshape(CH // 8, 8, TILE)
                    got = jnp.where((row8 == float(g + k))[None], piece, got)
            halves.append(got)
        got = (halves[0] + halves[1]).reshape(CH, TILE)
        jac = jnp.concatenate(
            [r32[pl.ds(at, LANES), :].T[0:CH], r32[pl.ds(at + LANES, LANES), :].T[0:CH]], axis=1
        )
        evolved = jnp.sum(jac * got, axis=0, keepdims=True)
        residual = weight * (evolved - value)
        yt[:, pl.ds(at, TILE)] = (jac * residual).astype(BF16)
        return carry

    lax.fori_loop(0, SLOTS // TILE, gather, 0)

    def scatter(g, carry):
        for k in range(GROUP):
            want = (g * GROUP + k).astype(F32)
            for c in range(0, SLOTS, 512):
                here = jnp.where(rowb[:, c : c + 512].astype(F32) == want, 1.0, 0.0).astype(BF16)
                part = yt[:, c : c + 512].reshape(CH // 16, 16, 512) * here[None]
                zt[k * CH : (k + 1) * CH, c : c + 512] = part.reshape(CH, 512)
        total = lax.dot_general(
            zt[...], ct[...], (((1,), (1,)), ((), ())), preferred_element_type=F32
        )
        for k in range(GROUP):
            forcing[g * GROUP + k] = total[k * CH : (k + 1) * CH]
        return carry

    lax.fori_loop(0, ROWS // GROUP, scatter, 0)
    wait(outgoing)


def vmem(n):
    return [pl.BlockSpec(memory_space=pltpu.VMEM)] * n


def anywhere(n):
    return [pl.BlockSpec(memory_space=pl.ANY)] * n


def params(**more):
    return pltpu.CompilerParams(vmem_limit_bytes=60 * 1024 * 1024, **more)


def advection_scratch(strip_rows):
    return [
        pltpu.VMEM((EXT, CH, RING), F32),
        pltpu.VMEM((EXT, CH, RING), F32),
        pltpu.VMEM((4, H, CH, COLS), BF16),
        pltpu.VMEM((7, strip_rows, LANES), F32),
    ]


def covariance_scratch(pattern_rows):
    return [
        pltpu.VMEM((pattern_rows, 32, BLOCK), F32),
        pltpu.VMEM((4 * CH, OFFS * BLOCK), BF16),
        pltpu.VMEM((OFFS * BLOCK, BLOCK), BF16),
    ]


def forward_call(ctrl, winds, pattern, cov):
    xa, xb, stage, strips = advection_scratch(CH + 8)
    return pl.pallas_call(
        forward_kernel,
        name="forward",
        out_shape=(
            jax.ShapeDtypeStruct((ROWS, CH, COLS), F32),
            jax.ShapeDtypeStruct((EXT, 8, RING), F32),
            jax.ShapeDtypeStruct((WIDE, 32, BLOCK), BF16),
        ),
        in_specs=anywhere(2) + vmem(2),
        out_specs=tuple(vmem(3)),
        scratch_shapes=[
            pltpu.VMEM((ROWS, CH, COLS), F32),
            pltpu.VMEM((WIDE, CH, COLS), BF16),
            pltpu.VMEM((WIDE, 32, BLOCK), BF16),
            *covariance_scratch(ROWS),
            xa,
            xb,
            stage,
            pltpu.VMEM((EXT, 8, RING), F32),
            strips,
            pltpu.SemaphoreType.DMA((2, 18)),
            pltpu.SemaphoreType.DMA((2, ROWS)),
        ],
        compiler_params=params(collective_id=0, has_side_effects=True),
        cost_estimate=pl.CostEstimate(
            flops=3_000_000_000, bytes_accessed=16_000_000, transcendentals=0
        ),
    )(ctrl, winds, pattern, cov)


def adjoint_call(forcing, winds, pattern, cov):
    xa, xb, stage, strips = advection_scratch(CH)
    return pl.pallas_call(
        adjoint_kernel,
        name="adjoint",
        out_shape=jax.ShapeDtypeStruct((CH, ROWS, COLS), F32),
        in_specs=vmem(4),
        out_specs=anywhere(1)[0],
        scratch_shapes=[
            pltpu.VMEM((WIDE, CH, COLS), BF16),
            *covariance_scratch(WIDE),
            xa,
            xb,
            stage,
            strips,
            pltpu.VMEM((ROWS, CH, COLS), F32),
            pltpu.SemaphoreType.DMA((2, 12)),
            pltpu.SemaphoreType.DMA((ROWS,)),
        ],
        compiler_params=params(collective_id=1, has_side_effects=True),
    )(forcing, winds, pattern, cov)


def obs_call(rec, fin):
    return pl.pallas_call(
        obs_kernel,
        name="observe",
        out_shape=(
            jax.ShapeDtypeStruct((ROWS, CH, COLS), F32),
            jax.ShapeDtypeStruct((CH, ROWS, COLS), F32),
        ),
        in_specs=vmem(1) + anywhere(1),
        out_specs=tuple(vmem(1) + anywhere(1)),
        scratch_shapes=[
            pltpu.VMEM((ROWS, CH, COLS), F32),
            pltpu.VMEM((2, ROWS * CH, COLS), BF16),
            pltpu.VMEM((SLOTS, LANES), F32),
            pltpu.VMEM((4, 32, LANES), F32),
            pltpu.VMEM((COLS, SLOTS), BF16),
            pltpu.VMEM((16, SLOTS), BF16),
            pltpu.VMEM((CH, SLOTS), BF16),
            pltpu.VMEM((GROUP * CH, SLOTS), BF16),
            pltpu.SemaphoreType.DMA((ROWS + 1,)),
        ],
        compiler_params=params(),
    )(rec, fin)


def on_device(
    control, winds, pattern, cov_tables, jacobians, obs_value, obs_weight, obs_column, obs_count
):
    slots = obs_column.shape[2]
    live = lax.broadcasted_iota(jnp.int32, obs_column.shape[1:], 1) < obs_count[0][:, None]
    weight = jnp.where(live, obs_weight[0], jnp.zeros((), BF16))
    row = (obs_column[0] // COLS).astype(BF16)
    col = (obs_column[0] % COLS).astype(BF16)
    extra = jnp.stack([obs_value[0], weight, row, col], axis=1)
    extra = jnp.pad(extra, ((0, 0), (0, slots - 4), (0, 0)))
    record = jnp.concatenate([jacobians[0], extra], axis=2)
    rec = lax.all_to_all(record, ("lat", "lon"), split_axis=0, concat_axis=0, tiled=True)

    rows_global = lax.axis_index("lat") * ROWS + jnp.arange(ROWS, dtype=jnp.int32)
    reached = rows_global[:, None] + jnp.arange(-R, R + 1, dtype=jnp.int32)[None, :]
    inside = (reached >= 0) & (reached < ROWS * lax.axis_size("lat"))
    mask = jnp.where(inside[:, None, :], pattern, 0)
    mask = jnp.pad(mask, ((0, 0), (0, 0), (0, 16 - OFFS))).reshape(ROWS, 32)
    mask = jnp.broadcast_to(mask.astype(BF16)[:, :, None], (ROWS, 32, BLOCK))

    wind2 = winds.reshape(2 * STEPS, ROWS, COLS)
    fin, wext, pext = forward_call(control, wind2, mask, cov_tables)
    forcing, forecast = obs_call(rec.reshape(SLOTS, LANES), fin)
    back = adjoint_call(forcing, wext, pext, cov_tables)
    return forecast, control + back


def solution(mesh):
    in_specs = (
        P(None, "lat", "lon"),
        P(None, None, "lat", "lon"),
        P("lat", "lon", None),
        P(),
        P(("lat", "lon"), None, None, None),
        P(("lat", "lon"), None, None),
        P(("lat", "lon"), None, None),
        P(("lat", "lon"), None, None),
        P(("lat", "lon"), None),
    )
    out_specs = (P(None, "lat", "lon"), P(None, "lat", "lon"))
    return jax.shard_map(
        on_device, mesh=mesh, in_specs=in_specs, out_specs=out_specs, check_vma=False
    )
```

time: 141 us -> 108 us (0.77)
  Pallas kernels: 118 us -> 85.5 us
  local copies, waits for them, and re-layouts: 7.11 us -> 4 us
  other arithmetic: 3.6 us -> 6.49 us
    pallas_call x1, Pallas kernels: 40.3 us -> 27.5 us  [adjoint_call(): pl.pallas_call(adjoint_kernel, name='adjoint', out_shape=jax.ShapeDtypeSt...]
    pallas_call x1, Pallas kernels: 50.4 us -> 40 us  [forward_call(): pl.pallas_call(forward_kernel, name='forward', out_shape=(jax.ShapeDtypeS...]
    pallas_call x1, Pallas kernels: 26.9 us -> 18.1 us  [obs_call(): pl.pallas_call(obs_kernel, name='observe', out_shape=(jax.ShapeDtypeStruc...]
    unnamed x13 -> x9, local copies, waits for them, and re-layouts: 6.21 us -> 3.11 us
    add x0 -> x1, other arithmetic: none -> 2.89 us  [on_device(): return (forecast, control + back)]
  transfers between devices with their start and end apart: 1 -> 1, of which waited for: 0 -> 0; matrix products, arithmetic and copies ran while one was open for 1% -> 1% of each run, Pallas kernels for 36% -> 37%
where the time goes in v1:
time: 108 us
  Pallas kernels  85.5 us (79%)
  starting transfers between devices  11.2 us (10%)
  other arithmetic  6.49 us (6%)
  local copies, waits for them, and re-layouts  4 us (4%)
    pallas_call x1, Pallas kernels, forward_call(): pl.pallas_call(forward_kernel, name='forward', out_shape=(jax.ShapeDtypeS...  40 us
    pallas_call x1, Pallas kernels, adjoint_call(): pl.pallas_call(adjoint_kernel, name='adjoint', out_shape=jax.ShapeDtypeSt...  27.5 us
    pallas_call x1, Pallas kernels, obs_call(): pl.pallas_call(obs_kernel, name='observe', out_shape=(jax.ShapeDtypeStruc...  18.1 us
    all_to_all x1, starting transfers between devices, on_device(): lax.all_to_all(record, ('lat', 'lon'), split_axis=0, concat_axis=0, tiled...  11.2 us
    unnamed x9, local copies, waits for them, and re-layouts  3.11 us
    add x1, other arithmetic, on_device(): return (forecast, control + back)  2.89 us
  transfers between devices with their start and end apart: 1, of which 0 were waited for; matrix products, arithmetic and copies ran while one was open for 1% of the time, Pallas kernels for 37%

profile of v1, /device:TPU:0, one launch (start us, length us, event | category | flops | bytes accessed | tf_op | source)
XLA Modules:
  0.0 107.9 jit_solution(4004160947508180276)
XLA Ops:
  0.6 0.7 fusion.2
  1.4 0.7 fusion.5
  2.1 0.7 pad_maximum_fusion
  2.8 0.1 copy.22
  2.9 1.9 %copy.19 = bf16[1,128,32,96]{3,2,1,0:T(8,128)(2,1)S(1)} copy(bf16[1,128,32,96]{1,3,2,0:T(8,128)(2,1)} %param.13) | data formatting | bytes 1572864 | tf_op args[4]
  4.8 1.4 %fusion.1 = bf16[128,32,128]{2,1,0:T(8,128)(2,1)} fusion(bf16[128,4,32]{2,1,0:T(4,128)(2,1)S(1)} %copy.22, bf16[128,32,96]{2,1,0:T(8,128)(2,1)S(1)} %bitcast.33), kind=kLoop, calls=%fused_computation.2 | loop fusion | flops 3145728 | bytes 1867776 | tf_op jit(solution)/shard_map/concatenate | solution.py:620
  6.2 0.0 copy-start.2
  6.2 11.2 %all-to-all-start = ((bf16[128,32,128]{2,1,0:T(8,128)(2,1)}), bf16[128,32,128]{2,1,0:T(8,128)(2,1)S(1)}, u32[]{:S(2)}, u32[]{:S(2)}) async-start(bf16[128,32,128]{2,1,0:T(8,128)(2,1)} %fusion.1), calls=%async_computation | async-start | bytes 2097152 | tf_op jit(solution)/shard_map/all_to_all | solution.py:621
  17.4 0.1 fusion.8
  17.5 0.0 copy-done.2
  17.5 0.1 copy.23
  17.6 0.1 convert_element_type.32
  17.7 0.8 broadcast_in_dim.28.pattern
  18.5 40.0 %forward.1 = (f32[16,96,256]{2,1,0:T(8,128)}, f32[24,8,384]{2,1,0:T(8,128)}, bf16[28,32,128]{2,1,0:T(8,128)(2,1)}) custom-call(f32[96,16,256]{2,1,0:T(8,128)} %ctrl.1, f32[8,16,256]{2,1,0:T(8,128)} %bitcast.37, bf16[16,32,128]{2,1,0:T(8,128)(2,1)} %broadcast_in_dim.28.pattern, bf16[7,128,128]{2,1,0:T(8,128)(2,1)} %cov.3), custom_call_target="tpu_custom_call" | custom-call | flops 3000000000 | bytes 16000000 | tf_op jit(solution)/shard_map/forward/pallas_call | solution.py:532
  58.5 0.0 all-to-all-done
  58.5 0.0 copy-start
  58.5 1.0 copy-done
  59.4 18.1 %observe.1 = (f32[16,96,256]{2,1,0:T(8,128)}, f32[96,16,256]{2,1,0:T(8,128)}) custom-call(bf16[4096,128]{1,0:T(8,128)(2,1)} %bitcast.34, f32[16,96,256]{2,1,0:T(8,128)} %get-tuple-element.7.fin), custom_call_target="tpu_custom_call" | custom-call | tf_op jit(solution)/shard_map/observe/pallas_call | solution.py:586
  77.5 0.0 copy-start.1
  77.5 27.5 %adjoint.1 = f32[96,16,256]{2,1,0:T(8,128)} custom-call(f32[16,96,256]{2,1,0:T(8,128)} %get-tuple-element.9.forcing, f32[24,8,384]{2,1,0:T(8,128)} %get-tuple-element.10.winds, bf16[28,32,128]{2,1,0:T(8,128)(2,1)} %get-tuple-element.11.pattern, bf16[7,128,128]{2,1,0:T(8,128)(2,1)} %cov.3), custom_call_target="tpu_custom_call" | custom-call | tf_op jit(solution)/shard_map/adjoint/pallas_call | solution.py:564
  105.0 0.0 copy-done.1
  105.0 2.9 %add.69 = f32[96,16,256]{2,1,0:T(8,128)} add(f32[96,16,256]{2,1,0:T(8,128)S(1)} %copy-done.1, f32[96,16,256]{2,1,0:T(8,128)} %adjoint.1) | non-fusion elementwise | flops 393216 | bytes 4718592 | tf_op jit(solution)/shard_map/add | solution.py:634
  (4 shorter events, 0.0 us)
Async XLA Ops:
  6.2 11.3 %copy-start.2 = (s32[16,2,13]{0,1,2:T(2,128)S(1)}, s32[16,2,13]{0,1,2:T(2,128)}, u32[]{:S(2)}) copy-start(s32[16,2,13]{0,1,2:T(2,128)} %param.11) | copy-start | bytes 4996
  6.2 52.3 %all-to-all-start = ((bf16[128,32,128]{2,1,0:T(8,128)(2,1)}), bf16[128,32,128]{2,1,0:T(8,128)(2,1)S(1)}, u32[]{:S(2)}, u32[]{:S(2)}) async-start(bf16[128,32,128]{2,1,0:T(8,128)(2,1)} %fusion.1), calls=%async_computation | async-start | bytes 2097152 | tf_op jit(solution)/shard_map/all_to_all | solution.py:621
  58.5 1.0 copy-start
  77.5 27.5 %copy-start.1 = (f32[96,16,256]{2,1,0:T(8,128)S(1)}, f32[96,16,256]{2,1,0:T(8,128)}, u32[]{:S(2)}) copy-start(f32[96,16,256]{2,1,0:T(8,128)} %ctrl.1) | copy-start | bytes 4718596

commit v2 on v1

--- a/solution.py
+++ b/solution.py
@@ -20,6 +20,7 @@
 SLOTS = 4096
 TILE = 256
 GROUP = 4
+WAVE = 49
 F32 = jnp.float32
 BF16 = jnp.bfloat16
 MESH = pl.DeviceIdType.MESH
@@ -39,6 +40,26 @@
     )
 
 
+def nth_peer(k):
+    n_lon = lax.axis_size("lon")
+    n = lax.axis_size("lat") * n_lon
+    other = lax.rem(lax.axis_index("lat") * n_lon + lax.axis_index("lon") + 45 * k, n)
+    return other, (lax.div(other, n_lon), lax.rem(other, n_lon))
+
+
+def greet_all():
+    barrier = pltpu.get_barrier_semaphore()
+    n = lax.axis_size("lat") * lax.axis_size("lon")
+
+    def signal(k, carry):
+        _, who = nth_peer(k)
+        pl.semaphore_signal(barrier, inc=1, device_id=who, device_id_type=MESH)
+        return carry
+
+    lax.fori_loop(1, n, signal, 0)
+    pl.semaphore_wait(barrier, n - 1)
+
+
 def greet():
     barrier = pltpu.get_barrier_semaphore()
     for who in neighbours():
@@ -214,7 +235,7 @@
             for k in range(OFFS):
                 at = base + n + (2 * R - k if adjoint else k)
                 at_pat = at if adjoint else base + n
-                mask = pat[at_pat, 16 * b + k : 16 * b + k + 1, :]
+                mask = pat[at_pat, 2 * k + b : 2 * k + b + 1, :]
                 mask = jnp.broadcast_to(mask, (16, BLOCK)).astype(BF16)
                 rows = ext[at, :, b * BLOCK : (b + 1) * BLOCK].reshape(CH // 16, 16, BLOCK)
                 lhs[m : m + CH, k * BLOCK : (k + 1) * BLOCK] = (rows * mask[None]).reshape(CH, BLOCK)
@@ -260,9 +281,82 @@
     )
 
 
+def pattern_table(pattern, table):
+    table[...] = jnp.zeros_like(table)
+    for k in range(OFFS):
+        table[2 * k : 2 * k + 2, 0:ROWS] = pattern[k].astype(F32)
+    shape = table.shape
+    offset = lax.broadcasted_iota(jnp.int32, shape, 0) // 2 - R
+    row = lax.axis_index("lat") * ROWS + lane_iota(shape) + offset
+    inside = (row >= 0) & (row < ROWS * lax.axis_size("lat"))
+    table[...] = jnp.where(inside, table[...], 0.0)
+
+
+def records(jac, value, weight, column, count, wide, packed):
+    slots = value.shape[0]
+    live = lax.broadcasted_iota(jnp.int32, value.shape, 0) < jnp.broadcast_to(count[...], value.shape)
+    cell = column[...]
+    extra = (
+        value[...].astype(F32),
+        jnp.where(live, weight[...].astype(F32), 0.0),
+        lax.shift_right_logical(cell, 8).astype(F32),
+        jnp.bitwise_and(cell, COLS - 1).astype(F32),
+    )
+
+    def put(s, low):
+        block = jnp.concatenate([jac[s].astype(F32), low], axis=0)
+        wide[pl.ds(s, LANES, stride=slots), :] = block.T
+
+    for s in range(4):
+        put(s, extra[s])
+
+    def rest(s, carry):
+        put(s, jnp.zeros(value.shape, F32))
+        return carry
+
+    lax.fori_loop(4, slots, rest, 0)
+
+    def narrow(t, carry):
+        at = pl.multiple_of(t * 512, 512)
+        packed[pl.ds(at, 512), :] = wide[pl.ds(at, 512), :].astype(BF16)
+        return carry
+
+    lax.fori_loop(0, SLOTS // 512, narrow, 0)
+
+
+def record_copy(packed, rec, sems, k):
+    per = SLOTS // (lax.axis_size("lat") * lax.axis_size("lon"))
+    me = lax.axis_index("lat") * lax.axis_size("lon") + lax.axis_index("lon")
+    other, who = nth_peer(k)
+    return pltpu.make_async_remote_copy(
+        src_ref=packed.at[pl.ds(pl.multiple_of(other * per, per), per)],
+        dst_ref=rec.at[pl.ds(pl.multiple_of(me * per, per), per)],
+        send_sem=sems.at[0, k],
+        recv_sem=sems.at[1, k],
+        device_id=who,
+        device_id_type=MESH,
+    )
+
+
+def send_records(packed, rec, sems, first, last):
+    def one(k, carry):
+        record_copy(packed, rec, sems, k).start()
+        return carry
+
+    lax.fori_loop(first, last, one, 0)
+
+
+def wait_records(packed, rec, sems):
+    def one(k, carry):
+        record_copy(packed, rec, sems, k).wait()
+        return carry
+
+    lax.fori_loop(1, lax.axis_size("lat") * lax.axis_size("lon"), one, 0)
+
+
 def forward_kernel(
-    ctrl, winds, pattern, cov, fin, wout, pout,
-    raw, ext, pext, pf, lhs, covcat, xa, xb, stage, wext, strips, sems, local,
+    ctrl, winds, pattern, cov, jac, value, weight, column, count, fin, wout, pout, rec,
+    raw, ext, tables, pf, lhs, covcat, xa, xb, stage, wext, strips, wide_rec, packed, sems, local, rsems,
 ):
     order = (14, 15, 0, 1, 12, 13, 2, 3, 10, 11, 4, 5, 6, 7, 8, 9)
     rows_in = {r: pltpu.make_async_copy(ctrl.at[:, r, :], raw.at[r], local.at[0, r]) for r in order}
@@ -274,7 +368,8 @@
         rows_in[r].start()
     for copy in winds_in:
         copy.start()
-    greet()
+    pattern_table(pattern, tables.at[0])
+    greet_all()
     chunks = []
     for n, (up, down) in enumerate(((14, 0), (12, 2), (10, 4))):
         for r in (up, up + 1, down, down + 1):
@@ -290,11 +385,22 @@
     for r in range(6, 10):
         rows_in[r].wait()
         ext[R + r] = raw[r].astype(BF16)
+    patterns = [
+        send(tables.at[0], tables.at[1], sems, 16, NORTH),
+        send(tables.at[0], tables.at[2], sems, 17, SOUTH),
+    ]
+    records(jac, value, weight, column, count, wide_rec, packed)
+    peers = lax.axis_size("lat") * lax.axis_size("lon")
+    per = SLOTS // peers
+    me = lax.axis_index("lat") * lax.axis_size("lon") + lax.axis_index("lon")
+    mine = pl.ds(pl.multiple_of(me * per, per), per)
+    own = pltpu.make_async_copy(packed.at[mine], rec.at[mine], local.at[2, 0])
+    own.start()
+    send_records(packed, rec, rsems, 1, WAVE)
     for k in range(OFFS):
         covcat[k * BLOCK : (k + 1) * BLOCK, :] = cov[abs(k - R)]
-    pf[...] = pattern[...].astype(F32)
     for r in range(ROWS):
-        pext[R + r] = pattern[r]
+        pf[r] = jnp.broadcast_to(tables[0, :, r : r + 1], (32, BLOCK))
 
     def pairs(first, gap):
         def pair(t, carry):
@@ -324,10 +430,7 @@
 
     wait(send_strips(strips, sems, 12, put))
     turned = send_corners(strips, sems, 14)
-    patterns = [
-        send(pext.at[pl.ds(ROWS, R)], pext.at[pl.ds(0, R)], sems, 16, NORTH),
-        send(pext.at[pl.ds(R, R)], pext.at[pl.ds(R + ROWS, R)], sems, 17, SOUTH),
-    ]
+    send_records(packed, rec, rsems, WAVE, peers)
     for rr in range(H, H + ROWS):
         xa[rr, :, COLS:RING] = own_halo(strips, 0, CH, rr)
         wext[rr, :, COLS:RING] = own_halo(strips, CH, CH + 8, rr)
@@ -349,13 +452,20 @@
     outer(forward_row, xa, xb, wext, steps, emit)
     wout[...] = wext[...]
     wait(patterns)
-    pout[...] = pext[...]
+    pout[...] = tables[...]
+    own.wait()
+    wait_records(packed, rec, rsems)
 
 
 def adjoint_kernel(
-    forcing, winds, pattern, cov, out,
+    forcing, winds, pattern, cov, ctrl, out,
     ext, pf, lhs, covcat, xa, xb, stage, strips, back, sems, local,
 ):
+    incoming = [
+        pltpu.make_async_copy(ctrl.at[:, r, :], back.at[r], local.at[1, r]) for r in range(ROWS)
+    ]
+    for copy in incoming:
+        copy.start()
     greet()
     xa[H : H + ROWS, :, 0:COLS] = forcing[...]
     rows = send_rows(xa, stage, sems, 0, 12, 0, 4, 0)
@@ -368,7 +478,10 @@
         turned = cov[k].astype(F32).T.astype(BF16)
         for at in {R + k, R - k}:
             covcat[at * BLOCK : (at + 1) * BLOCK, :] = turned
-    pf[...] = pattern[...].astype(F32)
+    for i in range(WIDE):
+        r = i - R
+        slot, lane = (1, r + ROWS) if r < 0 else (2, r - ROWS) if r >= ROWS else (0, r)
+        pf[i] = jnp.broadcast_to(pattern[slot, :, lane : lane + 1], (32, BLOCK))
     wait(sides)
     turned = send_corners(strips, sems, 4)
     for rr in range(H, H + ROWS):
@@ -392,6 +505,7 @@
     chunks.append(send_pair(ext, sems, 8, 14, 0))
     chunks.append(send_pair(ext, sems, 10, 12, 2))
     outgoing = []
+    wait(incoming)
 
     def pairs(first, gap):
         def pair(t, carry):
@@ -400,12 +514,13 @@
             for n in range(2):
                 for b in range(2):
                     m = (2 * n + b) * CH
-                    back[base + n, :, b * BLOCK : (b + 1) * BLOCK] = y[m : m + CH]
+                    lanes = slice(b * BLOCK, (b + 1) * BLOCK)
+                    back[base + n, :, lanes] = back[base + n, :, lanes] + y[m : m + CH]
             return carry
 
         lax.fori_loop(0, 2, pair, 0)
         for r in (first, first + 1, first + gap, first + gap + 1):
-            copy = pltpu.make_async_copy(back.at[r], out.at[:, r, :], local.at[r])
+            copy = pltpu.make_async_copy(back.at[r], out.at[:, r, :], local.at[0, r])
             copy.start()
             outgoing.append(copy)
 
@@ -527,7 +642,7 @@
     ]
 
 
-def forward_call(ctrl, winds, pattern, cov):
+def forward_call(*args):
     xa, xb, stage, strips = advection_scratch(CH + 8)
     return pl.pallas_call(
         forward_kernel,
@@ -535,37 +650,41 @@
         out_shape=(
             jax.ShapeDtypeStruct((ROWS, CH, COLS), F32),
             jax.ShapeDtypeStruct((EXT, 8, RING), F32),
-            jax.ShapeDtypeStruct((WIDE, 32, BLOCK), BF16),
+            jax.ShapeDtypeStruct((3, 32, LANES), F32),
+            jax.ShapeDtypeStruct((SLOTS, LANES), BF16),
         ),
-        in_specs=anywhere(2) + vmem(2),
-        out_specs=tuple(vmem(3)),
+        in_specs=anywhere(2) + vmem(7),
+        out_specs=tuple(vmem(3) + anywhere(1)),
         scratch_shapes=[
             pltpu.VMEM((ROWS, CH, COLS), F32),
             pltpu.VMEM((WIDE, CH, COLS), BF16),
-            pltpu.VMEM((WIDE, 32, BLOCK), BF16),
+            pltpu.VMEM((3, 32, LANES), F32),
             *covariance_scratch(ROWS),
             xa,
             xb,
             stage,
             pltpu.VMEM((EXT, 8, RING), F32),
             strips,
+            pltpu.VMEM((SLOTS, LANES), F32),
+            pltpu.VMEM((SLOTS, LANES), BF16),
             pltpu.SemaphoreType.DMA((2, 18)),
-            pltpu.SemaphoreType.DMA((2, ROWS)),
+            pltpu.SemaphoreType.DMA((3, ROWS)),
+            pltpu.SemaphoreType.DMA((2, 128)),
         ],
         compiler_params=params(collective_id=0, has_side_effects=True),
         cost_estimate=pl.CostEstimate(
             flops=3_000_000_000, bytes_accessed=16_000_000, transcendentals=0
         ),
-    )(ctrl, winds, pattern, cov)
-
-
-def adjoint_call(forcing, winds, pattern, cov):
+    )(*args)
+
+
+def adjoint_call(forcing, winds, pattern, cov, ctrl):
     xa, xb, stage, strips = advection_scratch(CH)
     return pl.pallas_call(
         adjoint_kernel,
         name="adjoint",
         out_shape=jax.ShapeDtypeStruct((CH, ROWS, COLS), F32),
-        in_specs=vmem(4),
+        in_specs=vmem(4) + anywhere(1),
         out_specs=anywhere(1)[0],
         scratch_shapes=[
             pltpu.VMEM((WIDE, CH, COLS), BF16),
@@ -576,10 +695,10 @@
             strips,
             pltpu.VMEM((ROWS, CH, COLS), F32),
             pltpu.SemaphoreType.DMA((2, 12)),
-            pltpu.SemaphoreType.DMA((ROWS,)),
+            pltpu.SemaphoreType.DMA((2, ROWS)),
         ],
         compiler_params=params(collective_id=1, has_side_effects=True),
-    )(forcing, winds, pattern, cov)
+    )(forcing, winds, pattern, cov, ctrl)
 
 
 def obs_call(rec, fin):
@@ -610,28 +729,21 @@
 def on_device(
     control, winds, pattern, cov_tables, jacobians, obs_value, obs_weight, obs_column, obs_count
 ):
-    slots = obs_column.shape[2]
-    live = lax.broadcasted_iota(jnp.int32, obs_column.shape[1:], 1) < obs_count[0][:, None]
-    weight = jnp.where(live, obs_weight[0], jnp.zeros((), BF16))
-    row = (obs_column[0] // COLS).astype(BF16)
-    col = (obs_column[0] % COLS).astype(BF16)
-    extra = jnp.stack([obs_value[0], weight, row, col], axis=1)
-    extra = jnp.pad(extra, ((0, 0), (0, slots - 4), (0, 0)))
-    record = jnp.concatenate([jacobians[0], extra], axis=2)
-    rec = lax.all_to_all(record, ("lat", "lon"), split_axis=0, concat_axis=0, tiled=True)
-
-    rows_global = lax.axis_index("lat") * ROWS + jnp.arange(ROWS, dtype=jnp.int32)
-    reached = rows_global[:, None] + jnp.arange(-R, R + 1, dtype=jnp.int32)[None, :]
-    inside = (reached >= 0) & (reached < ROWS * lax.axis_size("lat"))
-    mask = jnp.where(inside[:, None, :], pattern, 0)
-    mask = jnp.pad(mask, ((0, 0), (0, 0), (0, 16 - OFFS))).reshape(ROWS, 32)
-    mask = jnp.broadcast_to(mask.astype(BF16)[:, :, None], (ROWS, 32, BLOCK))
-
     wind2 = winds.reshape(2 * STEPS, ROWS, COLS)
-    fin, wext, pext = forward_call(control, wind2, mask, cov_tables)
-    forcing, forecast = obs_call(rec.reshape(SLOTS, LANES), fin)
-    back = adjoint_call(forcing, wext, pext, cov_tables)
-    return forecast, control + back
+    fin, wext, table, rec = forward_call(
+        control,
+        wind2,
+        jnp.transpose(pattern, (2, 1, 0)),
+        cov_tables,
+        jnp.transpose(jacobians[0], (1, 2, 0)),
+        obs_value[0].T,
+        obs_weight[0].T,
+        obs_column[0].T,
+        obs_count,
+    )
+    forcing, forecast = obs_call(rec, fin)
+    gradient = adjoint_call(forcing, wext, table, cov_tables, control)
+    return forecast, gradient
 
 
 def solution(mesh):

time: 108 us -> 97.9 us (0.906)
  starting transfers between devices: 11.2 us -> 0 us
  Pallas kernels: 85.5 us -> 94.3 us
  other arithmetic: 6.49 us -> 0 us
  local copies, waits for them, and re-layouts: 4 us -> 2.67 us
    all_to_all x1 -> x0, starting transfers between devices: 11.2 us -> none  [on_device(): lax.all_to_all(record, ('lat', 'lon'), split_axis=0, concat_axis=0, tiled...]
    pallas_call x1, Pallas kernels: 40 us -> 45.7 us  [forward_call(): pl.pallas_call(forward_kernel, name='forward', out_shape=(jax.ShapeDtypeS...]
    pallas_call x1, Pallas kernels: 27.5 us -> 30.5 us  [adjoint_call(): pl.pallas_call(adjoint_kernel, name='adjoint', out_shape=jax.ShapeDtypeSt...]
    add x3 -> x0, other arithmetic: 2.9 us -> none  [the longest x1 2.89 us: on_device(): return (forecast, control + back)]
    concatenate x1 -> x0, other arithmetic: 1.35 us -> none  [on_device(): record = jnp.concatenate([jacobians[0], extra], axis=2)]
    unnamed x9 -> x1, local copies, waits for them, and re-layouts: 3.11 us -> 2.67 us
  transfers between devices with their start and end apart: 1 -> 0, of which waited for: 0 -> 0; matrix products, arithmetic and copies ran while one was open for 1% -> 0% of each run, Pallas kernels for 37% -> 0%
where the time goes in v2:
time: 97.9 us; the launch traced here: 97.6 us
  Pallas kernels  94.3 us (96%)
  local copies, waits for them, and re-layouts  2.67 us (3%)
    pallas_call x1, Pallas kernels, forward_call(): pl.pallas_call(forward_kernel, name='forward', out_shape=(jax.ShapeDtypeS...  45.7 us
    pallas_call x1, Pallas kernels, adjoint_call(): pl.pallas_call(adjoint_kernel, name='adjoint', out_shape=jax.ShapeDtypeSt...  30.5 us
    pallas_call x1, Pallas kernels, obs_call(): pl.pallas_call(obs_kernel, name='observe', out_shape=(jax.ShapeDtypeStruc...  18.1 us
    unnamed x1, local copies, waits for them, and re-layouts  2.67 us

profile of v2, /device:TPU:0, one launch (start us, length us, event | category | flops | bytes accessed | tf_op | source)
XLA Modules:
  0.0 97.6 jit_solution(13091638889996637136)
XLA Ops:
  0.6 45.7 %forward.1 = (f32[16,96,256]{2,1,0:T(8,128)}, f32[24,8,384]{2,1,0:T(8,128)}, f32[3,32,128]{2,1,0:T(8,128)}, bf16[4096,128]{1,0:T(8,128)(2,1)}) custom-call(f32[96,16,256]{2,1,0:T(8,128)} %ctrl.3, f32[8,16,256]{2,1,0:T(8,128)} %bitcast.15, s32[13,2,16]{2,1,0:T(2,128)} %bitcast.17, bf16[7,128,128]{2,1,0:T(8,128)(2,1)} %cov.3, bf16[32,96,128]{2,1,0:T(8,128)(2,1)} %bitcast.14, ...), custom_call_target="tpu_custom_call" | custom-call | flops 3000000000 | bytes 16000000 | tf_op jit(solution)/shard_map/forward/pallas_call | solution.py:647
  46.3 18.1 %observe.1 = (f32[16,96,256]{2,1,0:T(8,128)}, f32[96,16,256]{2,1,0:T(8,128)}) custom-call(bf16[4096,128]{1,0:T(8,128)(2,1)} %get-tuple-element.8.rec, f32[16,96,256]{2,1,0:T(8,128)} %get-tuple-element.9.fin), custom_call_target="tpu_custom_call" | custom-call | tf_op jit(solution)/shard_map/observe/pallas_call | solution.py:705
  64.4 30.5 %adjoint.1 = f32[96,16,256]{2,1,0:T(8,128)} custom-call(f32[16,96,256]{2,1,0:T(8,128)} %get-tuple-element.11.forcing, f32[24,8,384]{2,1,0:T(8,128)} %get-tuple-element.12.winds, f32[3,32,128]{2,1,0:T(8,128)} %get-tuple-element.13.pattern, bf16[7,128,128]{2,1,0:T(8,128)(2,1)} %cov.3, f32[96,16,256]{2,1,0:T(8,128)} %ctrl.3), custom_call_target="tpu_custom_call" | custom-call | tf_op jit(solution)/shard_map/adjoint/pallas_call | solution.py:683
  94.9 2.7 %copy.12 = f32[96,16,256]{2,1,0:T(8,128)} copy(f32[96,16,256]{2,1,0:T(8,128)} %adjoint.1) | data formatting | bytes 3145728

commit v3 on v2

--- a/solution.py
+++ b/solution.py
@@ -40,31 +40,47 @@
     )
 
 
-def nth_peer(k):
-    n_lon = lax.axis_size("lon")
-    n = lax.axis_size("lat") * n_lon
-    other = lax.rem(lax.axis_index("lat") * n_lon + lax.axis_index("lon") + 45 * k, n)
-    return other, (lax.div(other, n_lon), lax.rem(other, n_lon))
+STRIDE = 45
+
+
+def peer_count():
+    return lax.axis_size("lat") * lax.axis_size("lon")
+
+
+def own_number():
+    return lax.axis_index("lat") * lax.axis_size("lon") + lax.axis_index("lon")
+
+
+def for_peers(first, last, do):
+    n = peer_count()
+
+    def one(k, other):
+        do(other)
+        other = other + STRIDE
+        return jnp.where(other >= n, other - n, other)
+
+    lax.fori_loop(first, last, one, lax.rem(own_number() + STRIDE * first, n))
 
 
 def greet_all():
     barrier = pltpu.get_barrier_semaphore()
-    n = lax.axis_size("lat") * lax.axis_size("lon")
-
-    def signal(k, carry):
-        _, who = nth_peer(k)
-        pl.semaphore_signal(barrier, inc=1, device_id=who, device_id_type=MESH)
-        return carry
-
-    lax.fori_loop(1, n, signal, 0)
-    pl.semaphore_wait(barrier, n - 1)
+
+    def signal(other):
+        pl.semaphore_signal(
+            barrier, inc=1, device_id=other, device_id_type=pl.DeviceIdType.LOGICAL
+        )
+
+    for_peers(1, peer_count(), signal)
 
 
 def greet():
     barrier = pltpu.get_barrier_semaphore()
     for who in neighbours():
         pl.semaphore_signal(barrier, inc=1, device_id=who, device_id_type=MESH)
-    pl.semaphore_wait(barrier, 4)
+
+
+def greeted(count):
+    pl.semaphore_wait(pltpu.get_barrier_semaphore(), count)
 
 
 def send(src, dst, sems, index, side):
@@ -324,34 +340,34 @@
     lax.fori_loop(0, SLOTS // 512, narrow, 0)
 
 
-def record_copy(packed, rec, sems, k):
-    per = SLOTS // (lax.axis_size("lat") * lax.axis_size("lon"))
-    me = lax.axis_index("lat") * lax.axis_size("lon") + lax.axis_index("lon")
-    other, who = nth_peer(k)
+def record_copy(packed, rec, sems, other):
+    per = SLOTS // peer_count()
     return pltpu.make_async_remote_copy(
         src_ref=packed.at[pl.ds(pl.multiple_of(other * per, per), per)],
-        dst_ref=rec.at[pl.ds(pl.multiple_of(me * per, per), per)],
-        send_sem=sems.at[0, k],
-        recv_sem=sems.at[1, k],
-        device_id=who,
+        dst_ref=rec.at[pl.ds(pl.multiple_of(own_number() * per, per), per)],
+        send_sem=sems.at[0],
+        recv_sem=sems.at[1],
+        device_id=other,
+        device_id_type=pl.DeviceIdType.LOGICAL,
+    )
+
+
+def send_records(packed, rec, sems, first, last):
+    for_peers(first, last, lambda other: record_copy(packed, rec, sems, other).start())
+
+
+def wait_records(packed, rec, sems):
+    most = pl.ds(0, SLOTS - SLOTS // peer_count())
+    both = pltpu.make_async_remote_copy(
+        src_ref=packed.at[most],
+        dst_ref=rec.at[most],
+        send_sem=sems.at[0],
+        recv_sem=sems.at[1],
+        device_id=neighbours()[0],
         device_id_type=MESH,
     )
-
-
-def send_records(packed, rec, sems, first, last):
-    def one(k, carry):
-        record_copy(packed, rec, sems, k).start()
-        return carry
-
-    lax.fori_loop(first, last, one, 0)
-
-
-def wait_records(packed, rec, sems):
-    def one(k, carry):
-        record_copy(packed, rec, sems, k).wait()
-        return carry
-
-    lax.fori_loop(1, lax.axis_size("lat") * lax.axis_size("lon"), one, 0)
+    both.wait_send()
+    both.wait_recv()
 
 
 def forward_kernel(
@@ -359,6 +375,7 @@
     raw, ext, tables, pf, lhs, covcat, xa, xb, stage, wext, strips, wide_rec, packed, sems, local, rsems,
 ):
     order = (14, 15, 0, 1, 12, 13, 2, 3, 10, 11, 4, 5, 6, 7, 8, 9)
+    greet_all()
     rows_in = {r: pltpu.make_async_copy(ctrl.at[:, r, :], raw.at[r], local.at[0, r]) for r in order}
     winds_in = [
         pltpu.make_async_copy(winds.at[:, r, :], wext.at[H + r, :, pl.ds(0, COLS)], local.at[1, r])
@@ -369,38 +386,34 @@
     for copy in winds_in:
         copy.start()
     pattern_table(pattern, tables.at[0])
-    greet_all()
-    chunks = []
-    for n, (up, down) in enumerate(((14, 0), (12, 2), (10, 4))):
-        for r in (up, up + 1, down, down + 1):
-            rows_in[r].wait()
-            ext[R + r] = raw[r].astype(BF16)
-        chunks.append(send_pair(ext, sems, 2 * n, up, down))
+    for r in order:
+        rows_in[r].wait()
+        ext[R + r] = raw[r].astype(BF16)
+    for k in range(OFFS):
+        covcat[k * BLOCK : (k + 1) * BLOCK, :] = cov[abs(k - R)]
+    for r in range(ROWS):
+        pf[r] = jnp.broadcast_to(tables[0, :, r : r + 1], (32, BLOCK))
     wait(winds_in)
+    greeted(peer_count() - 1)
+    chunks = [
+        send_pair(ext, sems, 2 * n, up, down)
+        for n, (up, down) in enumerate(((14, 0), (12, 2), (10, 4)))
+    ]
     wide = pl.ds(0, COLS)
     wind_rows_sent = (
         send(wext.at[pl.ds(ROWS, H), :, wide], wext.at[pl.ds(0, H), :, wide], sems, 6, NORTH),
         send(wext.at[pl.ds(H, H), :, wide], wext.at[pl.ds(ROWS + H, H), :, wide], sems, 7, SOUTH),
     )
-    for r in range(6, 10):
-        rows_in[r].wait()
-        ext[R + r] = raw[r].astype(BF16)
     patterns = [
         send(tables.at[0], tables.at[1], sems, 16, NORTH),
         send(tables.at[0], tables.at[2], sems, 17, SOUTH),
     ]
     records(jac, value, weight, column, count, wide_rec, packed)
-    peers = lax.axis_size("lat") * lax.axis_size("lon")
-    per = SLOTS // peers
-    me = lax.axis_index("lat") * lax.axis_size("lon") + lax.axis_index("lon")
-    mine = pl.ds(pl.multiple_of(me * per, per), per)
+    per = SLOTS // peer_count()
+    mine = pl.ds(pl.multiple_of(own_number() * per, per), per)
     own = pltpu.make_async_copy(packed.at[mine], rec.at[mine], local.at[2, 0])
     own.start()
     send_records(packed, rec, rsems, 1, WAVE)
-    for k in range(OFFS):
-        covcat[k * BLOCK : (k + 1) * BLOCK, :] = cov[abs(k - R)]
-    for r in range(ROWS):
-        pf[r] = jnp.broadcast_to(tables[0, :, r : r + 1], (32, BLOCK))
 
     def pairs(first, gap):
         def pair(t, carry):
@@ -430,30 +443,39 @@
 
     wait(send_strips(strips, sems, 12, put))
     turned = send_corners(strips, sems, 14)
-    send_records(packed, rec, rsems, WAVE, peers)
+    send_records(packed, rec, rsems, WAVE, peer_count())
     for rr in range(H, H + ROWS):
         xa[rr, :, COLS:RING] = own_halo(strips, 0, CH, rr)
         wext[rr, :, COLS:RING] = own_halo(strips, CH, CH + 8, rr)
 
     def emit(rr):
         def put(c, low, high):
-            fin[rr - H, c : c + 8, :] = low[:, 0:COLS]
-            fin[rr - H, c + 8 : c + 16, :] = high[:, 0:COLS]
+            raw[rr - H, c : c + 8, :] = low[:, 0:COLS]
+            raw[rr - H, c + 8 : c + 16, :] = high[:, 0:COLS]
 
         return put
+
+    def put_out(first, count, index):
+        here = pl.ds(first, count)
+        copy = pltpu.make_async_copy(raw.at[here], fin.at[here], local.at[2, index])
+        copy.start()
+        return copy
 
     steps = tuple(range(STEPS))
     inner(forward_row, xa, xb, wext, steps, emit)
+    outgoing = [put_out(4, 8, 1)]
     wait(near + far + turned + wind_rows_sent)
     place_rows(xa, stage, (0, 1, 2, 3), (2, 3, 0, 1))
     for rr in (*range(H), *range(H + ROWS, EXT)):
         xa[rr, :, COLS:RING] = corner_halo(strips, 0, CH, rr) * row_valid(rr)
         wext[rr, :, COLS:RING] = corner_halo(strips, CH, CH + 8, rr)
     outer(forward_row, xa, xb, wext, steps, emit)
+    outgoing += [put_out(0, 4, 2), put_out(12, 4, 3)]
     wout[...] = wext[...]
     wait(patterns)
     pout[...] = tables[...]
     own.wait()
+    wait(outgoing)
     wait_records(packed, rec, rsems)
 
 
@@ -464,16 +486,26 @@
     incoming = [
         pltpu.make_async_copy(ctrl.at[:, r, :], back.at[r], local.at[1, r]) for r in range(ROWS)
     ]
-    for copy in incoming:
+    greet()
+    fields = [
+        pltpu.make_async_copy(
+            forcing.at[pl.ds(first, count)],
+            xa.at[pl.ds(H + first, count), :, pl.ds(0, COLS)],
+            local.at[2, first],
+        )
+        for first, count in ((12, 4), (0, 4), (4, 8))
+    ]
+    for copy in fields + incoming:
         copy.start()
-    greet()
-    xa[H : H + ROWS, :, 0:COLS] = forcing[...]
+    wait(fields)
+    strips[0] = pack_strip(lambda rr: xa[rr, :, COLS - LANES : COLS], LANES - H)
+    strips[1] = pack_strip(lambda rr: xa[rr, :, 0:LANES], 0)
+    greeted(4)
+    sides = (
+        send(strips.at[0], strips.at[2], sems, 2, EAST),
+        send(strips.at[1], strips.at[3], sems, 3, WEST),
+    )
     rows = send_rows(xa, stage, sems, 0, 12, 0, 4, 0)
-
-    def put(slot, at, first):
-        strips[slot] = pack_strip(lambda rr: xa[rr, :, at : at + LANES], first)
-
-    sides = send_strips(strips, sems, 2, put)
     for k in range(R + 1):
         turned = cov[k].astype(F32).T.astype(BF16)
         for at in {R + k, R - k}:
@@ -594,6 +626,7 @@
         return carry
 
     lax.fori_loop(0, SLOTS // TILE, gather, 0)
+    wait(outgoing)
 
     def scatter(g, carry):
         for k in range(GROUP):
@@ -606,11 +639,16 @@
             zt[...], ct[...], (((1,), (1,)), ((), ())), preferred_element_type=F32
         )
         for k in range(GROUP):
-            forcing[g * GROUP + k] = total[k * CH : (k + 1) * CH]
+            field[g * GROUP + k] = total[k * CH : (k + 1) * CH]
+        put_out(g).start()
         return carry
 
+    def put_out(g):
+        here = pl.ds(g * GROUP, GROUP)
+        return pltpu.make_async_copy(field.at[here], forcing.at[here], local.at[g])
+
     lax.fori_loop(0, ROWS // GROUP, scatter, 0)
-    wait(outgoing)
+    wait([put_out(g) for g in range(ROWS // GROUP)])
 
 
 def vmem(n):
@@ -654,7 +692,7 @@
             jax.ShapeDtypeStruct((SLOTS, LANES), BF16),
         ),
         in_specs=anywhere(2) + vmem(7),
-        out_specs=tuple(vmem(3) + anywhere(1)),
+        out_specs=tuple(anywhere(1) + vmem(2) + anywhere(1)),
         scratch_shapes=[
             pltpu.VMEM((ROWS, CH, COLS), F32),
             pltpu.VMEM((WIDE, CH, COLS), BF16),
@@ -669,7 +707,7 @@
             pltpu.VMEM((SLOTS, LANES), BF16),
             pltpu.SemaphoreType.DMA((2, 18)),
             pltpu.SemaphoreType.DMA((3, ROWS)),
-            pltpu.SemaphoreType.DMA((2, 128)),
+            pltpu.SemaphoreType.DMA((2,)),
         ],
         compiler_params=params(collective_id=0, has_side_effects=True),
         cost_estimate=pl.CostEstimate(
@@ -684,7 +722,7 @@
         adjoint_kernel,
         name="adjoint",
         out_shape=jax.ShapeDtypeStruct((CH, ROWS, COLS), F32),
-        in_specs=vmem(4) + anywhere(1),
+        in_specs=anywhere(1) + vmem(3) + anywhere(1),
         out_specs=anywhere(1)[0],
         scratch_shapes=[
             pltpu.VMEM((WIDE, CH, COLS), BF16),
@@ -695,7 +733,7 @@
             strips,
             pltpu.VMEM((ROWS, CH, COLS), F32),
             pltpu.SemaphoreType.DMA((2, 12)),
-            pltpu.SemaphoreType.DMA((2, ROWS)),
+            pltpu.SemaphoreType.DMA((3, ROWS)),
         ],
         compiler_params=params(collective_id=1, has_side_effects=True),
     )(forcing, winds, pattern, cov, ctrl)
@@ -710,7 +748,7 @@
             jax.ShapeDtypeStruct((CH, ROWS, COLS), F32),
         ),
         in_specs=vmem(1) + anywhere(1),
-        out_specs=tuple(vmem(1) + anywhere(1)),
+        out_specs=tuple(anywhere(2)),
         scratch_shapes=[
             pltpu.VMEM((ROWS, CH, COLS), F32),
             pltpu.VMEM((2, ROWS * CH, COLS), BF16),

time: 97.9 us -> 93 us (0.950)
  Pallas kernels: 94.3 us -> 89.3 us
    pallas_call x1, Pallas kernels: 45.7 us -> 42.1 us  [forward_call(): pl.pallas_call(forward_kernel, name='forward', out_shape=(jax.ShapeDtypeS...]
    pallas_call x1, Pallas kernels: 30.5 us -> 29.6 us  [adjoint_call(): pl.pallas_call(adjoint_kernel, name='adjoint', out_shape=jax.ShapeDtypeSt...]
where the time goes in v3:
time: 93 us; the launch traced here: 92.6 us
  Pallas kernels  89.3 us (96%)
  local copies, waits for them, and re-layouts  2.67 us (3%)
    pallas_call x1, Pallas kernels, forward_call(): pl.pallas_call(forward_kernel, name='forward', out_shape=(jax.ShapeDtypeS...  42.1 us
    pallas_call x1, Pallas kernels, adjoint_call(): pl.pallas_call(adjoint_kernel, name='adjoint', out_shape=jax.ShapeDtypeSt...  29.6 us
    pallas_call x1, Pallas kernels, obs_call(): pl.pallas_call(obs_kernel, name='observe', out_shape=(jax.ShapeDtypeStruc...  17.7 us
    unnamed x1, local copies, waits for them, and re-layouts  2.67 us

profile of v3, /device:TPU:0, one launch (start us, length us, event | category | flops | bytes accessed | tf_op | source)
XLA Modules:
  0.0 92.6 jit_solution(188810316531257858)
XLA Ops:
  0.6 42.1 %forward.1 = (f32[16,96,256]{2,1,0:T(8,128)}, f32[24,8,384]{2,1,0:T(8,128)}, f32[3,32,128]{2,1,0:T(8,128)}, bf16[4096,128]{1,0:T(8,128)(2,1)}) custom-call(f32[96,16,256]{2,1,0:T(8,128)} %ctrl.3, f32[8,16,256]{2,1,0:T(8,128)} %bitcast.15, s32[13,2,16]{2,1,0:T(2,128)} %bitcast.17, bf16[7,128,128]{2,1,0:T(8,128)(2,1)} %cov.3, bf16[32,96,128]{2,1,0:T(8,128)(2,1)} %bitcast.14, ...), custom_call_target="tpu_custom_call" | custom-call | flops 3000000000 | bytes 16000000 | tf_op jit(solution)/shard_map/forward/pallas_call | solution.py:685
  42.7 17.7 %observe.1 = (f32[16,96,256]{2,1,0:T(8,128)}, f32[96,16,256]{2,1,0:T(8,128)}) custom-call(bf16[4096,128]{1,0:T(8,128)(2,1)} %get-tuple-element.8.rec, f32[16,96,256]{2,1,0:T(8,128)} %get-tuple-element.9.fin), custom_call_target="tpu_custom_call" | custom-call | tf_op jit(solution)/shard_map/observe/pallas_call | solution.py:743
  60.4 29.6 %adjoint.1 = f32[96,16,256]{2,1,0:T(8,128)} custom-call(f32[16,96,256]{2,1,0:T(8,128)} %get-tuple-element.11.forcing, f32[24,8,384]{2,1,0:T(8,128)} %get-tuple-element.12.winds, f32[3,32,128]{2,1,0:T(8,128)} %get-tuple-element.13.pattern, bf16[7,128,128]{2,1,0:T(8,128)(2,1)} %cov.3, f32[96,16,256]{2,1,0:T(8,128)} %ctrl.3), custom_call_target="tpu_custom_call" | custom-call | tf_op jit(solution)/shard_map/adjoint/pallas_call | solution.py:721
  90.0 2.7 %copy.12 = f32[96,16,256]{2,1,0:T(8,128)} copy(f32[96,16,256]{2,1,0:T(8,128)} %adjoint.1) | data formatting | bytes 3145728

commit v4 on v3

--- a/solution.py
+++ b/solution.py
@@ -20,7 +20,6 @@
 SLOTS = 4096
 TILE = 256
 GROUP = 4
-WAVE = 49
 F32 = jnp.float32
 BF16 = jnp.bfloat16
 MESH = pl.DeviceIdType.MESH
@@ -206,7 +205,7 @@
         emit(c, part(c), part(c + 8))
 
 
-def advance(row, src, dst, wext, step, pairs, base, emit=None):
+def advance(row, src, dst, wext, step, turns, per, base, emit=None):
     def store(rr):
         def put(c, low, high):
             dst[rr, c : c + 8, :] = low
@@ -215,12 +214,12 @@
         return put
 
     def body(t, carry):
-        for k in range(2):
+        for k in range(per):
             rr = base(t) + k
             row(src, wext, rr, step, (emit or store)(rr))
         return carry
 
-    lax.fori_loop(0, pairs, body, 0)
+    lax.fori_loop(0, turns, body, 0)
 
 
 def inner(row, xa, xb, wext, steps, emit):
@@ -228,7 +227,12 @@
     for n in range(STEPS):
         first = H + 1 + n
         last = emit if n == STEPS - 1 else None
-        advance(row, src, dst, wext, steps[n], 7 - n, lambda t, first=first: first + 2 * t, last)
+        count = ROWS - 2 - 2 * n
+        per = 4 if count % 4 == 0 else 2
+        advance(
+            row, src, dst, wext, steps[n], count // per, per,
+            lambda t, first=first, per=per: first + per * t, last,
+        )
         src, dst = dst, src
 
 
@@ -238,8 +242,8 @@
         low, high = 1 + n, H + ROWS - 1 - n
         last = emit if n == STEPS - 1 else None
         advance(
-            row, src, dst, wext, steps[n], 4,
-            lambda t, low=low, high=high: 2 * t + jnp.where(t < 2, low, high - 4), last,
+            row, src, dst, wext, steps[n], 2, 4,
+            lambda t, low=low, high=high: low + t * (high - low), last,
         )
         src, dst = dst, src
 
@@ -375,7 +379,6 @@
     raw, ext, tables, pf, lhs, covcat, xa, xb, stage, wext, strips, wide_rec, packed, sems, local, rsems,
 ):
     order = (14, 15, 0, 1, 12, 13, 2, 3, 10, 11, 4, 5, 6, 7, 8, 9)
-    greet_all()
     rows_in = {r: pltpu.make_async_copy(ctrl.at[:, r, :], raw.at[r], local.at[0, r]) for r in order}
     winds_in = [
         pltpu.make_async_copy(winds.at[:, r, :], wext.at[H + r, :, pl.ds(0, COLS)], local.at[1, r])
@@ -385,6 +388,7 @@
         rows_in[r].start()
     for copy in winds_in:
         copy.start()
+    greet_all()
     pattern_table(pattern, tables.at[0])
     for r in order:
         rows_in[r].wait()
@@ -413,19 +417,15 @@
     mine = pl.ds(pl.multiple_of(own_number() * per, per), per)
     own = pltpu.make_async_copy(packed.at[mine], rec.at[mine], local.at[2, 0])
     own.start()
-    send_records(packed, rec, rsems, 1, WAVE)
 
     def pairs(first, gap):
-        def pair(t, carry):
+        for t in range(2):
             base = first + gap * t
-            y = cov_pair(base, ext, pf, lhs, covcat, False)
+            y = cov_pair(base, ext, pf, lhs.at[t], covcat, False)
             for n in range(2):
                 for b in range(2):
                     m = (2 * n + b) * CH
                     xa[H + base + n, :, b * BLOCK : (b + 1) * BLOCK] = y[m : m + CH]
-            return carry
-
-        lax.fori_loop(0, 2, pair, 0)
 
     pairs(6, 2)
     wait(chunks[0])
@@ -443,7 +443,7 @@
 
     wait(send_strips(strips, sems, 12, put))
     turned = send_corners(strips, sems, 14)
-    send_records(packed, rec, rsems, WAVE, peer_count())
+    send_records(packed, rec, rsems, 1, peer_count())
     for rr in range(H, H + ROWS):
         xa[rr, :, COLS:RING] = own_halo(strips, 0, CH, rr)
         wext[rr, :, COLS:RING] = own_halo(strips, CH, CH + 8, rr)
@@ -540,17 +540,14 @@
     wait(incoming)
 
     def pairs(first, gap):
-        def pair(t, carry):
+        for t in range(2):
             base = first + gap * t
-            y = cov_pair(base, ext, pf, lhs, covcat, True)
+            y = cov_pair(base, ext, pf, lhs.at[t], covcat, True)
             for n in range(2):
                 for b in range(2):
                     m = (2 * n + b) * CH
                     lanes = slice(b * BLOCK, (b + 1) * BLOCK)
                     back[base + n, :, lanes] = back[base + n, :, lanes] + y[m : m + CH]
-            return carry
-
-        lax.fori_loop(0, 2, pair, 0)
         for r in (first, first + 1, first + gap, first + gap + 1):
             copy = pltpu.make_async_copy(back.at[r], out.at[:, r, :], local.at[0, r])
             copy.start()
@@ -599,7 +596,7 @@
     def vector(k, t):
         return jnp.concatenate([aux[k, pl.ds(2 * t, 1), :], aux[k, pl.ds(2 * t + 1, 1), :]], axis=1)
 
-    def gather(t, carry):
+    def gather(t):
         at = pl.multiple_of(t * TILE, TILE)
         value, weight, row, col = (vector(k, t) for k in range(4))
         hot = jnp.where(jnp.broadcast_to(col, (COLS, TILE)) == sub, 1.0, 0.0).astype(BF16)
@@ -623,14 +620,18 @@
         evolved = jnp.sum(jac * got, axis=0, keepdims=True)
         residual = weight * (evolved - value)
         yt[:, pl.ds(at, TILE)] = (jac * residual).astype(BF16)
+
+    def two_tiles(t, carry):
+        gather(2 * t)
+        gather(2 * t + 1)
         return carry
 
-    lax.fori_loop(0, SLOTS // TILE, gather, 0)
+    lax.fori_loop(0, SLOTS // TILE // 2, two_tiles, 0)
     wait(outgoing)
 
-    def scatter(g, carry):
+    def scatter(g, zt):
         for k in range(GROUP):
-            want = (g * GROUP + k).astype(F32)
+            want = float(g * GROUP + k)
             for c in range(0, SLOTS, 512):
                 here = jnp.where(rowb[:, c : c + 512].astype(F32) == want, 1.0, 0.0).astype(BF16)
                 part = yt[:, c : c + 512].reshape(CH // 16, 16, 512) * here[None]
@@ -641,13 +642,13 @@
         for k in range(GROUP):
             field[g * GROUP + k] = total[k * CH : (k + 1) * CH]
         put_out(g).start()
-        return carry
 
     def put_out(g):
         here = pl.ds(g * GROUP, GROUP)
         return pltpu.make_async_copy(field.at[here], forcing.at[here], local.at[g])
 
-    lax.fori_loop(0, ROWS // GROUP, scatter, 0)
+    for g in range(ROWS // GROUP):
+        scatter(g, zt.at[g % 2])
     wait([put_out(g) for g in range(ROWS // GROUP)])
 
 
@@ -675,7 +676,7 @@
 def covariance_scratch(pattern_rows):
     return [
         pltpu.VMEM((pattern_rows, 32, BLOCK), F32),
-        pltpu.VMEM((4 * CH, OFFS * BLOCK), BF16),
+        pltpu.VMEM((2, 4 * CH, OFFS * BLOCK), BF16),
         pltpu.VMEM((OFFS * BLOCK, BLOCK), BF16),
     ]
 
@@ -739,6 +740,38 @@
     )(forcing, winds, pattern, cov, ctrl)
 
 
+PIECES = 8
+
+
+def copy_kernel(field, out, held, sems):
+    share = CH // PIECES
+    pieces = [pl.ds(n * share, share) for n in range(PIECES)]
+    inward = [own_copy(field.at[p], held.at[p], sems.at[0, n]) for n, p in enumerate(pieces)]
+    outward = []
+    for n, p in enumerate(pieces):
+        inward[n].wait()
+        outward.append(own_copy(held.at[p], out.at[p], sems.at[1, n]))
+    wait(outward)
+
+
+def own_copy(src, dst, sem):
+    copy = pltpu.make_async_copy(src, dst, sem)
+    copy.start()
+    return copy
+
+
+def copy_call(field):
+    return pl.pallas_call(
+        copy_kernel,
+        name="copy_out",
+        out_shape=jax.ShapeDtypeStruct((CH, ROWS, COLS), F32),
+        in_specs=anywhere(1),
+        out_specs=anywhere(1)[0],
+        scratch_shapes=[pltpu.VMEM((CH, ROWS, COLS), F32), pltpu.SemaphoreType.DMA((2, PIECES))],
+        compiler_params=params(),
+    )(field)
+
+
 def obs_call(rec, fin):
     return pl.pallas_call(
         obs_kernel,
@@ -757,7 +790,7 @@
             pltpu.VMEM((COLS, SLOTS), BF16),
             pltpu.VMEM((16, SLOTS), BF16),
             pltpu.VMEM((CH, SLOTS), BF16),
-            pltpu.VMEM((GROUP * CH, SLOTS), BF16),
+            pltpu.VMEM((2, GROUP * CH, SLOTS), BF16),
             pltpu.SemaphoreType.DMA((ROWS + 1,)),
         ],
         compiler_params=params(),
@@ -781,7 +814,7 @@
     )
     forcing, forecast = obs_call(rec, fin)
     gradient = adjoint_call(forcing, wext, table, cov_tables, control)
-    return forecast, gradient
+    return forecast, copy_call(gradient)
 
 
 def solution(mesh):

time: 93 us -> 87.7 us (0.943)
  Pallas kernels: 89.3 us -> 86.6 us
  local copies, waits for them, and re-layouts: 2.67 us -> 0 us
    pallas_call x1, Pallas kernels: 29.6 us -> 25.7 us  [adjoint_call(): pl.pallas_call(adjoint_kernel, name='adjoint', out_shape=jax.ShapeDtypeSt...]
    unnamed x1 -> x0, local copies, waits for them, and re-layouts: 2.67 us -> none
    pallas_call x0 -> x1, Pallas kernels: none -> 2.29 us  [copy_call(): pl.pallas_call(copy_kernel, name='copy_out', out_shape=jax.ShapeDtypeStru...]
    pallas_call x1, Pallas kernels: 17.7 us -> 15.9 us  [obs_call(): pl.pallas_call(obs_kernel, name='observe', out_shape=(jax.ShapeDtypeStruc...]
where the time goes in v4:
time: 87.7 us; the launch traced here: 87.4 us
  Pallas kernels  86.6 us (99%)
    pallas_call x1, Pallas kernels, forward_call(): pl.pallas_call(forward_kernel, name='forward', out_shape=(jax.ShapeDtypeS...  42.8 us
    pallas_call x1, Pallas kernels, adjoint_call(): pl.pallas_call(adjoint_kernel, name='adjoint', out_shape=jax.ShapeDtypeSt...  25.7 us
    pallas_call x1, Pallas kernels, obs_call(): pl.pallas_call(obs_kernel, name='observe', out_shape=(jax.ShapeDtypeStruc...  15.9 us
    pallas_call x1, Pallas kernels, copy_call(): pl.pallas_call(copy_kernel, name='copy_out', out_shape=jax.ShapeDtypeStru...  2.29 us

profile of v4, /device:TPU:0, one launch (start us, length us, event | category | flops | bytes accessed | tf_op | source)
XLA Modules:
  0.0 87.4 jit_solution(15640604510265926229)
XLA Ops:
  0.6 42.8 %forward.1 = (f32[16,96,256]{2,1,0:T(8,128)}, f32[24,8,384]{2,1,0:T(8,128)}, f32[3,32,128]{2,1,0:T(8,128)}, bf16[4096,128]{1,0:T(8,128)(2,1)}) custom-call(f32[96,16,256]{2,1,0:T(8,128)} %ctrl.3, f32[8,16,256]{2,1,0:T(8,128)} %bitcast.15, s32[13,2,16]{2,1,0:T(2,128)} %bitcast.17, bf16[7,128,128]{2,1,0:T(8,128)(2,1)} %cov.3, bf16[32,96,128]{2,1,0:T(8,128)(2,1)} %bitcast.14, ...), custom_call_target="tpu_custom_call" | custom-call | flops 3000000000 | bytes 16000000 | tf_op jit(solution)/shard_map/forward/pallas_call | solution.py:686
  43.4 15.9 %observe.1 = (f32[16,96,256]{2,1,0:T(8,128)}, f32[96,16,256]{2,1,0:T(8,128)}) custom-call(bf16[4096,128]{1,0:T(8,128)(2,1)} %get-tuple-element.8.rec, f32[16,96,256]{2,1,0:T(8,128)} %get-tuple-element.9.fin), custom_call_target="tpu_custom_call" | custom-call | tf_op jit(solution)/shard_map/observe/pallas_call | solution.py:776
  59.3 25.7 %adjoint.1.field = f32[96,16,256]{2,1,0:T(8,128)} custom-call(f32[16,96,256]{2,1,0:T(8,128)} %get-tuple-element.11.forcing, f32[24,8,384]{2,1,0:T(8,128)} %get-tuple-element.12.winds, f32[3,32,128]{2,1,0:T(8,128)} %get-tuple-element.13.pattern, bf16[7,128,128]{2,1,0:T(8,128)(2,1)} %cov.3, f32[96,16,256]{2,1,0:T(8,128)} %ctrl.3), custom_call_target="tpu_custom_call" | custom-call | tf_op jit(solution)/shard_map/adjoint/pallas_call | solution.py:722
  85.0 2.3 %copy_out.1 = f32[96,16,256]{2,1,0:T(8,128)} custom-call(f32[96,16,256]{2,1,0:T(8,128)} %adjoint.1.field), custom_call_target="tpu_custom_call" | custom-call | tf_op jit(solution)/shard_map/copy_out/pallas_call | solution.py:764

commit v5 on v4

--- a/solution.py
+++ b/solution.py
@@ -621,12 +621,12 @@
         residual = weight * (evolved - value)
         yt[:, pl.ds(at, TILE)] = (jac * residual).astype(BF16)
 
-    def two_tiles(t, carry):
-        gather(2 * t)
-        gather(2 * t + 1)
+    def four_tiles(t, carry):
+        for n in range(4):
+            gather(4 * t + n)
         return carry
 
-    lax.fori_loop(0, SLOTS // TILE // 2, two_tiles, 0)
+    lax.fori_loop(0, SLOTS // TILE // 4, four_tiles, 0)
     wait(outgoing)
 
     def scatter(g, zt):

time: 87.7 us -> 87.1 us (level)
  no operation moved by 1% of the time
where the time goes in v5:
time: 87.1 us; the launch traced here: 86.9 us
  Pallas kernels  86.1 us (99%)
    pallas_call x1, Pallas kernels, forward_call(): pl.pallas_call(forward_kernel, name='forward', out_shape=(jax.ShapeDtypeS...  42.8 us
    pallas_call x1, Pallas kernels, adjoint_call(): pl.pallas_call(adjoint_kernel, name='adjoint', out_shape=jax.ShapeDtypeSt...  25.7 us
    pallas_call x1, Pallas kernels, obs_call(): pl.pallas_call(obs_kernel, name='observe', out_shape=(jax.ShapeDtypeStruc...  15.3 us
    pallas_call x1, Pallas kernels, copy_call(): pl.pallas_call(copy_kernel, name='copy_out', out_shape=jax.ShapeDtypeStru...  2.29 us

profile of v5, /device:TPU:0, one launch (start us, length us, event | category | flops | bytes accessed | tf_op | source)
XLA Modules:
  0.0 86.9 jit_solution(14463726508629908620)
XLA Ops:
  0.6 42.8 %forward.1 = (f32[16,96,256]{2,1,0:T(8,128)}, f32[24,8,384]{2,1,0:T(8,128)}, f32[3,32,128]{2,1,0:T(8,128)}, bf16[4096,128]{1,0:T(8,128)(2,1)}) custom-call(f32[96,16,256]{2,1,0:T(8,128)} %ctrl.3, f32[8,16,256]{2,1,0:T(8,128)} %bitcast.15, s32[13,2,16]{2,1,0:T(2,128)} %bitcast.17, bf16[7,128,128]{2,1,0:T(8,128)(2,1)} %cov.3, bf16[32,96,128]{2,1,0:T(8,128)(2,1)} %bitcast.14, ...), custom_call_target="tpu_custom_call" | custom-call | flops 3000000000 | bytes 16000000 | tf_op jit(solution)/shard_map/forward/pallas_call | solution.py:686
  43.4 15.3 %observe.1 = (f32[16,96,256]{2,1,0:T(8,128)}, f32[96,16,256]{2,1,0:T(8,128)}) custom-call(bf16[4096,128]{1,0:T(8,128)(2,1)} %get-tuple-element.8.rec, f32[16,96,256]{2,1,0:T(8,128)} %get-tuple-element.9.fin), custom_call_target="tpu_custom_call" | custom-call | tf_op jit(solution)/shard_map/observe/pallas_call | solution.py:776
  58.8 25.7 %adjoint.1.field = f32[96,16,256]{2,1,0:T(8,128)} custom-call(f32[16,96,256]{2,1,0:T(8,128)} %get-tuple-element.11.forcing, f32[24,8,384]{2,1,0:T(8,128)} %get-tuple-element.12.winds, f32[3,32,128]{2,1,0:T(8,128)} %get-tuple-element.13.pattern, bf16[7,128,128]{2,1,0:T(8,128)(2,1)} %cov.3, f32[96,16,256]{2,1,0:T(8,128)} %ctrl.3), custom_call_target="tpu_custom_call" | custom-call | tf_op jit(solution)/shard_map/adjoint/pallas_call | solution.py:722
  84.4 2.3 %copy_out.1 = f32[96,16,256]{2,1,0:T(8,128)} custom-call(f32[96,16,256]{2,1,0:T(8,128)} %adjoint.1.field), custom_call_target="tpu_custom_call" | custom-call | tf_op jit(solution)/shard_map/copy_out/pallas_call | solution.py:764
